TPU v7x, 256 devices: a whole 4x4x8 slice. The times are simulated.
256 devices in a mesh: clus: 32 (over y, z), tgt: 8 (over x, core).
Axes of the slice: x: 4, y: 4, z: 8, core: 2. Of those that a mesh axis runs over, the one named last changes fastest.
Arguments:
- weights_init: float32 [262144, 1024], P('clus', 'tgt'), may hold values from -6 to 6
- margins: float32 [4096, 1024], P('clus', 'tgt')
- block_bits: int32 [9216, 128, 8], P('clus'), may hold values from 0 to 65535
- block_run_index: int32 [9216], P('clus'), may hold values from 0 to 31, as said below
- block_col: int32 [9216], P('clus'), may hold values from 0 to 63
- block_tally: int32 [32], P('clus'), may hold values from 144 to 288, as said below
- step_size: float32 [1], replicated, may hold values from 0.3 to 0.6
- penalty: float32 [1], replicated, may hold values from 0.3 to 0.8
Outputs:
- weights: float32 [262144, 1024], P('clus', 'tgt')
- run_loss: float32 [4096], P('clus')
Inputs may be any that keep to these rules, and one draw needn't show every extreme that they name: `block_run_index`: A device's slots name distinct pairs of run block and cluster block. `block_tally`: some device's list is full in every draw.
All inputs are finite; a program needn't handle non-finite values.
Results may differ from a plain program's by a relative error of at most 0.0025.
Values may be sent and summed in bfloat16 or wider, within the bound.
No kernel may reach another device: no remote copies, remote signals or barrier semaphores. Data moves between devices by JAX's collectives and lax.ppermute only.
A program may use at most 128 MiB of HBM per device.

v0:
```python
import math

import jax
import jax.numpy as jnp
from jax import lax
from jax.sharding import PartitionSpec as P

BLOCK_ENTRIES = 128
TARGETS = 1024
ITERS = 2


def pick_blocks(index, count, table):
    selector = (index[:, None] == jnp.arange(count, dtype=jnp.int32)[None, :]).astype(table.dtype)
    flat = table.reshape(count, -1)
    picked = jnp.dot(selector, flat, preferred_element_type=jnp.float32).astype(table.dtype)
    return picked.reshape((index.shape[0],) + table.shape[1:])


def add_blocks(total, index, values):
    count = total.shape[0]
    selector = (jnp.arange(count, dtype=jnp.int32)[:, None] == index[None, :]).astype(jnp.float32)
    flat = values.reshape(index.shape[0], -1)
    summed = jnp.dot(
        selector, flat, preferred_element_type=jnp.float32, precision=lax.Precision.HIGHEST
    )
    return total + summed.reshape(total.shape)


def per_device(
    weights_init, margins, block_bits, block_run_index, block_col, block_tally, step_size, penalty
):
    slot_total = block_run_index.shape[0]
    nblocks = weights_init.shape[0] // BLOCK_ENTRIES
    tcols = weights_init.shape[1]
    ndev = lax.axis_size("clus")
    group_index = math.gcd(slot_total, 36)
    rotation_turns = slot_total // group_index
    live_slots = (jnp.arange(slot_total, dtype=jnp.int32) < block_tally[0]).astype(jnp.bfloat16)
    shifts = jnp.arange(16, dtype=jnp.int32)
    packed_flags = jnp.right_shift(block_bits[..., None], shifts) & 1
    sign_values = (2 * packed_flags - 1).astype(jnp.bfloat16).reshape(
        slot_total, BLOCK_ENTRIES, BLOCK_ENTRIES
    ) * live_slots[:, None, None]
    sign_groups = sign_values.reshape(rotation_turns, group_index, BLOCK_ENTRIES, BLOCK_ENTRIES)
    place_groups = block_run_index.reshape(rotation_turns, group_index)
    col_groups = block_col.reshape(rotation_turns, group_index)
    eta = step_size[0]
    thresh = eta * penalty[0]
    current = weights_init
    err = jnp.zeros((BLOCK_ENTRIES, tcols), jnp.float32)
    for step in range(ITERS):
        current_b = current.astype(jnp.bfloat16).reshape(nblocks, BLOCK_ENTRIES, tcols)

        def forward(total, portion):
            scan_inputs, pos, cols = portion
            selected_block = pick_blocks(cols, nblocks, current_b)
            product_rows = jnp.einsum(
                "vjs,vsh->vjh", scan_inputs, selected_block, preferred_element_type=jnp.float32
            )
            return (add_blocks(total, pos, product_rows), None)

        total, unused = lax.scan(
            forward,
            jnp.zeros((ndev, BLOCK_ENTRIES, tcols), jnp.float32),
            (sign_groups, place_groups, col_groups),
        )
        owned = lax.psum_scatter(
            total.reshape(ndev * BLOCK_ENTRIES, tcols).astype(jnp.bfloat16),
            "clus",
            scatter_dimension=0,
            tiled=True,
        ).astype(jnp.float32)
        err = owned / 128.0 - margins
        err_b = err.astype(jnp.bfloat16)
        residual_table = lax.all_gather(err_b, "clus", axis=0, tiled=True).reshape(
            ndev, BLOCK_ENTRIES, tcols
        )

        def backward(total, portion):
            scan_inputs, pos, cols = portion
            design_rows = pick_blocks(pos, ndev, residual_table)
            part = jnp.einsum(
                "oeq,oei->oqi", scan_inputs, design_rows, preferred_element_type=jnp.float32
            )
            return (add_blocks(total, cols, part), None)

        grads, unused = lax.scan(
            backward,
            jnp.zeros((nblocks, BLOCK_ENTRIES, tcols), jnp.float32),
            (sign_groups, place_groups, col_groups),
        )
        grad = grads.reshape(nblocks * BLOCK_ENTRIES, tcols) / 128.0
        moved = current - eta * grad
        current = jnp.sign(moved) * jnp.maximum(jnp.abs(moved) - thresh, 0.0)
    squares = jnp.sum(err * err, axis=1)
    run_loss = lax.psum(squares, "tgt") / TARGETS
    return (current, run_loss)


def solution(mesh):
    return jax.shard_map(
        per_device,
        mesh=mesh,
        in_specs=(
            P("clus", "tgt"),
            P("clus", "tgt"),
            P("clus", None, None),
            P("clus"),
            P("clus"),
            P("clus"),
            P(),
            P(),
        ),
        out_specs=(P("clus", "tgt"), P("clus")),
        check_vma=False,
    )
```

profile of v0, /device:TPU:2, one launch (start us, length us, event | category | flops | bytes accessed | tf_op | source)
XLA Modules:
  0.0 1006.4 jit_solution(12187850462215080191)
XLA Ops:
  8.0 9.2 shift_right_arithmetic.21
  17.2 14.9 %fusion.60 = bf16[8,36,128,128]{2,3,1,0:T(8,128)(2,1)} fusion(s32[8,36,128,128]{2,3,1,0:T(8,128)} %bitcast.215, s32[128]{0:T(128)S(1)} %shift_right_arithmetic.24, bf16[8,36]{1,0:T(8,128)(2,1)S(1)} %fusion.63), kind=kLoop, calls=%fused_computation.77 | loop fusion | flops 42467328 | bytes 28312640 | tf_op jit(solution)/shard_map/mul | solution.py:42
  32.1 12.7 %copy.20 = bf16[8,36,128,128]{3,2,1,0:T(8,128)(2,1)} copy(bf16[8,36,128,128]{2,3,1,0:T(8,128)(2,1)} %fusion.60) | data formatting | bytes 18874368
  45.0 2.4 convert_element_type.64
  47.4 2.7 reshape_reshape.16
  50.0 80.1 %while.48 = (s32[]{:T(128)}, f32[32,128,128]{2,0,1:T(8,128)}, s32[8,36]{1,0:T(8,128)S(1)}, bf16[8,36,128,128]{3,2,1,0:T(8,128)(2,1)}, s32[8,36]{1,0:T(8,128)S(1)...) while((s32[]{:T(128)}, f32[32,128,128]{2,0,1:T(8,128)}, ...), condition=%wide.wide.region_1.2_spmd.clone, body=%wide.wide.region_0.1_spmd.clone.sunk | while | flops 454626688 | bytes 21890508 | solution.py:63
  50.0 2.1 convolution_convert_fusion.12
  54.5 4.2 select_add_fusion.12
  58.7 2.1 convolution_convert_fusion.12
  63.1 5.7 select_add_fusion.12
  68.9 2.1 convolution_convert_fusion.12
  73.3 5.7 select_add_fusion.12
  79.1 2.1 convolution_convert_fusion.12
  83.6 5.7 select_add_fusion.12
  89.3 2.1 convolution_convert_fusion.12
  93.8 5.7 select_add_fusion.12
  99.5 2.1 convolution_convert_fusion.12
  104.0 5.7 select_add_fusion.12
  109.7 2.1 convolution_convert_fusion.12
  114.2 5.7 select_add_fusion.12
  120.0 2.1 convolution_convert_fusion.12
  124.4 5.7 select_add_fusion.12
  133.5 220.0 %reduce-scatter.3.cloned.1.call-done = bf16[128,128]{1,0:T(8,128)(2,1)} async-done(((bf16[4096,128]{1,0:T(8,128)(2,1)}), bf16[128,128]{1,0:T(8,128)(2,1)}) %reduce-scatter.3.cloned.1.call-update) | async-done | bytes 32784 | tf_op jit(solution)/shard_map/reduce_scatter | solution.py:68
  356.4 74.3 %all-gather.3.cloned.1.call-done = bf16[4096,128]{1,0:T(8,128)(2,1)} async-done(((bf16[128,128]{1,0:T(8,128)(2,1)}), bf16[4096,128]{1,0:T(8,128)(2,1)}) %all-gather.3.cloned.1.call-update) | async-done | bytes 1048592 | tf_op jit(solution)/shard_map/all_gather | solution.py:76
  432.3 83.9 %while.49 = (s32[]{:T(128)}, f32[64,128,128]{2,0,1:T(8,128)}, s32[8,36]{1,0:T(8,128)S(1)}, bf16[8,36,128,128]{2,3,1,0:T(8,128)(2,1)}, s32[8,36]{1,0:T(8,128)S(1)...) while((s32[]{:T(128)}, f32[64,128,128]{2,0,1:T(8,128)}, ...), condition=%wide.wide.region_4.5_spmd.clone, body=%wide.wide.region_3.4_spmd.clone.sunk | while | flops 644418944 | bytes 25036236 | solution.py:88
  435.2 5.7 select_add_fusion.13
  443.8 7.9 select_add_fusion.13
  454.5 7.9 select_add_fusion.13
  465.3 7.9 select_add_fusion.13
  476.1 7.9 select_add_fusion.13
  486.8 7.9 select_add_fusion.13
  497.6 7.9 select_add_fusion.13
  508.3 7.9 select_add_fusion.13
  516.2 2.6 broadcast_multiply_fusion.1
  518.9 2.4 copy.22
  525.2 2.7 reshape_reshape.20
  527.9 80.0 %while.50 = (s32[]{:T(128)}, f32[32,128,128]{2,0,1:T(8,128)}, s32[8,36]{1,0:T(8,128)S(1)}, bf16[8,36,128,128]{3,2,1,0:T(8,128)(2,1)}, s32[8,36]{1,0:T(8,128)S(1)...) while((s32[]{:T(128)}, f32[32,128,128]{2,0,1:T(8,128)}, ...), condition=%wide.wide.region_6.7_spmd.clone, body=%wide.wide.region_5.6_spmd.clone.sunk | while | flops 454626688 | bytes 21890508 | solution.py:63
  527.9 2.1 convolution_convert_fusion.14
  532.4 4.1 select_add_fusion.14
  536.5 2.1 convolution_convert_fusion.14
  541.0 5.7 select_add_fusion.14
  546.7 2.1 convolution_convert_fusion.14
  551.2 5.7 select_add_fusion.14
  556.9 2.1 convolution_convert_fusion.14
  561.4 5.7 select_add_fusion.14
  571.6 5.7 select_add_fusion.14
  581.8 5.7 select_add_fusion.14
  592.0 5.7 select_add_fusion.14
  602.2 5.7 select_add_fusion.14
  611.2 214.7 %reduce-scatter.5.cloned.1.call-done = bf16[128,128]{1,0:T(8,128)(2,1)} async-done(((bf16[4096,128]{1,0:T(8,128)(2,1)}), bf16[128,128]{1,0:T(8,128)(2,1)}) %reduce-scatter.5.cloned.1.call-update) | async-done | bytes 32784 | tf_op jit(solution)/shard_map/reduce_scatter | solution.py:68
  827.3 10.2 %psum.7 = f32[128]{0:T(128)S(1)} all-reduce(f32[128]{0:T(128)S(1)} %get-tuple-element.298), channel_id=1, replica_groups=mesh['clus'=32,'tgt'=8] {'tgt'}, use_global_device_ids=true, to_apply=%region_11.12 | all-reduce | flops 128 | bytes 1024 | tf_op jit(solution)/shard_map/psum | solution.py:97
  838.0 65.1 %all-gather.5.cloned.1.call-done = bf16[4096,128]{1,0:T(8,128)(2,1)} async-done(((bf16[128,128]{1,0:T(8,128)(2,1)}), bf16[4096,128]{1,0:T(8,128)(2,1)}) %all-gather.5.cloned.1.call-update) | async-done | bytes 1048592 | tf_op jit(solution)/shard_map/all_gather | solution.py:76
  904.6 83.9 %while.51 = (s32[]{:T(128)}, f32[64,128,128]{2,0,1:T(8,128)}, s32[8,36]{1,0:T(8,128)S(1)}, bf16[8,36,128,128]{2,3,1,0:T(8,128)(2,1)}, s32[8,36]{1,0:T(8,128)S(1)...) while((s32[]{:T(128)}, f32[64,128,128]{2,0,1:T(8,128)}, ...), condition=%wide.wide.region_9.10_spmd.clone, body=%wide.wide.region_8.9_spmd.clone.sunk | while | flops 644418944 | bytes 25036236 | solution.py:88
  907.5 5.7 select_add_fusion.15
  916.1 7.9 select_add_fusion.15
  926.8 7.9 select_add_fusion.15
  937.6 7.9 select_add_fusion.15
  948.4 7.9 select_add_fusion.15
  959.1 7.9 select_add_fusion.15
  969.9 7.9 select_add_fusion.15
  980.6 7.9 select_add_fusion.15
  988.5 2.6 broadcast_multiply_fusion
  991.2 2.4 copy.25
  994.6 5.3 maximum_multiply_fusion
  (193 shorter events, 109.0 us)
Async XLA Ops:
  7.2 346.3 %reduce-scatter.3.cloned.1.call-start = ((), (), s32[]{:S(2)}) async-start(), calls=%async_computation.2 | async-start | bytes 1081344 | tf_op jit(solution)/shard_map/reduce_scatter | solution.py:68
  32.1 12.7 %copy-start.7 = (s32[288]{0:T(512)S(1)}, s32[288]{0:T(512)}, u32[]{:S(2)}) copy-start(s32[288]{0:T(512)} %param.20) | copy-start | bytes 3460
  32.1 12.8 %copy-start.8 = (s32[288]{0:T(512)S(1)}, s32[288]{0:T(512)}, u32[]{:S(2)}) copy-start(s32[288]{0:T(512)} %param.19) | copy-start | bytes 3460
  47.4 2.7 copy-start.4
  130.2 223.3 %copy-start.6 = (f32[128,128]{1,0:T(8,128)S(1)}, f32[128,128]{1,0:T(8,128)}, u32[]{:S(2)}) copy-start(f32[128,128]{1,0:T(8,128)} %param.17) | copy-start | bytes 196612
  133.4 297.4 %all-gather.3.cloned.1.call-start = ((), (), s32[]{:S(2)}) async-start(), calls=%async_computation.3 | async-start | bytes 1081344 | tf_op jit(solution)/shard_map/all_gather | solution.py:76
  354.9 471.0 %reduce-scatter.5.cloned.1.call-start = ((), (), s32[]{:S(2)}) async-start(), calls=%async_computation.4 | async-start | bytes 1081344 | tf_op jit(solution)/shard_map/reduce_scatter | solution.py:68
  518.9 4.6 copy-start
  521.3 2.1 copy-start.2
  525.2 2.7 copy-start.5
  611.1 292.0 %all-gather.5.cloned.1.call-start = ((), (), s32[]{:S(2)}) async-start(), calls=%async_computation.5 | async-start | bytes 1081344 | tf_op jit(solution)/shard_map/all_gather | solution.py:76
  991.2 2.5 copy-start.1
  991.2 3.5 copy-start.3
Sparse Core Ops, SparseCore 0:
  133.5 219.8 reduce-scatter.2
  356.1 74.6 all-gather.2
  611.2 214.5 reduce-scatter.4
  828.3 74.7 all-gather.4
where the time goes:
time: 1010 us
  waiting for transfers between devices  574 us (57%)
  matrix products  309 us (31%)
  local copies, waits for them, and re-layouts  59.1 us (6%)
  other arithmetic  36.5 us (4%)
  between operations  15.9 us (2%)
  blocking collectives  10.2 us (1%)
    reduce_scatter x2, waiting for transfers between devices, per_device(): lax.psum_scatter(total.reshape(ndev * BLOCK_ENTRIES, tcols).astype(jnp.bf...  435 us
    dot_general x32, matrix products, add_blocks(): jnp.dot(selector, flat, preferred_element_type=jnp.float32, precision=lax...  211 us
    all_gather x2, waiting for transfers between devices, per_device(): lax.all_gather(err_b, 'clus', axis=0, tiled=True)  139 us
    dot_general x32, matrix products, pick_blocks(): jnp.dot(selector, flat, preferred_element_type=jnp.float32)  43 us
    dot_general x16, matrix products, forward(): jnp.einsum('vjs,vsh->vjh', scan_inputs, selected_block, preferred_element...  27.8 us
    dot_general x16, matrix products, backward(): jnp.einsum('oeq,oei->oqi', scan_inputs, design_rows, preferred_element_ty...  27.8 us
  transfers between devices with their start and end apart: 4, of which 4 were waited for; matrix products, arithmetic and copies ran while one was open for 0% of the time, Pallas kernels for 0%

commit v1 on v0

v1 whole, which is shorter than its diff:
```python
import functools

import jax
import jax.numpy as jnp
from jax import lax
from jax.experimental import pallas as pl
from jax.experimental.pallas import tpu as pltpu
from jax.sharding import PartitionSpec as P


B = 128
TARGETS = 1024
NY = 4
NZ = 8
UNROLL = 4
CHUNK = 8
FAR = 2
MIB = 1024 * 1024
DZ_SLOT = (0, 2, 6, 5, 1, 3, 7, 4)


def shift(x, dy, dz):
    pairs = [
        (y * NZ + z, ((y + dy) % NY) * NZ + (z + dz) % NZ)
        for y in range(NY)
        for z in range(NZ)
    ]
    return lax.ppermute(x, "clus", pairs)


def build_lists(run, col, tally):
    slots = run.shape[0]
    nrun = NY * NZ
    me = lax.axis_index("clus")
    dy = (run // NZ - me // NZ) % NY
    dz = (run % NZ - me % NZ) % NZ
    place = jnp.zeros_like(dz)
    for k, s in enumerate(DZ_SLOT):
        place = place + jnp.where(dz == k, s, 0)
    ids = jnp.arange(slots, dtype=jnp.int32)
    live = ids < tally[0]
    rel = jnp.where(live, dy * NZ + place, nrun)
    blocks = jnp.arange(nrun, dtype=jnp.int32)
    hot = (rel[:, None] == blocks[None, :]).astype(jnp.int32)
    pairs = (jnp.sum(hot, axis=0) + 1) // 2
    before = (blocks[None, :] < blocks[:, None]).astype(jnp.int32)
    first = jnp.sum(before * pairs[None, :], axis=1)
    rank = jnp.sum(
        ((rel[None, :] == rel[:, None]) & (ids[None, :] < ids[:, None])).astype(jnp.int32), axis=1
    )
    pos = jnp.where(live, 2 * jnp.sum(hot * first[None, :], axis=1) + rank, -1)
    max_pairs = (slots + nrun) // 2 + UNROLL
    where = jnp.arange(2 * max_pairs, dtype=jnp.int32)
    code = ids + col * 512 + 32768
    codes = jnp.sum(jnp.where(where[:, None] == pos[None, :], code[None, :], 0), axis=1)
    last = first + pairs
    order = jnp.arange(max_pairs, dtype=jnp.int32)
    owner = jnp.sum((order[:, None] >= last[None, :]).astype(jnp.int32), axis=1)
    owner = jnp.minimum(owner, nrun - 1)
    bounds = jnp.concatenate([first[::NZ], jnp.sum(pairs)[None]])
    return codes.astype(jnp.int32), owner.astype(jnp.int32), bounds.astype(jnp.int32)


def unpack(bits_ref, masks, slot, mag):
    words = bits_ref[slot]
    parts = []
    for w in range(8):
        row = jnp.broadcast_to(words[w : w + 1, :], (16, B))
        parts.append(jnp.where((row & masks) != 0, mag, -mag).astype(jnp.bfloat16))
    return jnp.concatenate(parts, axis=0)


def bit_masks():
    return jnp.left_shift(jnp.int32(1), lax.broadcasted_iota(jnp.int32, (16, B), 0))


def load_pair(codes_ref, bits_ref, masks, q, high):
    signs, cols = [], []
    for h in range(2):
        code = codes_ref[2 * q + h]
        mag = jnp.where(q < high, lax.shift_right_logical(code, 15), 0).astype(jnp.float32)
        signs.append(unpack(bits_ref, masks, code & 511, mag))
        cols.append(lax.shift_right_logical(code, 9) & 63)
    return jnp.concatenate(signs, axis=0), cols


def each_pair(bounds_ref, group, body):
    low, high = bounds_ref[group], bounds_ref[group + 1]

    def step(k, carry):
        body([low + k * UNROLL + u for u in range(UNROLL)], high)
        return carry

    lax.fori_loop(0, (high - low + UNROLL - 1) // UNROLL, step, 0)


def forward(codes_ref, owner_ref, bounds_ref, bits_ref, cur_b, groups, outs):
    pl.run_scoped(
        functools.partial(
            forward_groups, codes_ref, owner_ref, bounds_ref, bits_ref, cur_b, groups, outs
        ),
        pltpu.VMEM((NZ, B, B), jnp.float32),
    )


def forward_groups(codes_ref, owner_ref, bounds_ref, bits_ref, cur_b, groups, outs, total):
    masks = bit_masks()
    for group, out in zip(groups, outs):
        total[...] = jnp.zeros_like(total)

        def body(qs, high):
            products = []
            for q in qs:
                signs, cols = load_pair(codes_ref, bits_ref, masks, q, high)
                left = jnp.concatenate([cur_b[cols[0]], cur_b[cols[1]]], axis=1)
                products.append(jnp.dot(left, signs, preferred_element_type=jnp.float32))
            for q, product in zip(qs, products):
                row = owner_ref[q] & (NZ - 1)
                total[row] = total[row] + product

        each_pair(bounds_ref, group, body)
        out[...] = total[...].astype(jnp.bfloat16)


def backward(codes_ref, owner_ref, bounds_ref, bits_ref, errs, grad):
    masks = bit_masks()
    grad[...] = jnp.zeros_like(grad)
    for group in range(NY):

        def body(qs, high):
            products, places = [], []
            for q in qs:
                signs, cols = load_pair(codes_ref, bits_ref, masks, q, high)
                row = errs[group][owner_ref[q] & (NZ - 1)]
                products.append(
                    lax.dot_general(
                        row, signs, (((1,), (1,)), ((), ())), preferred_element_type=jnp.float32
                    )
                )
                places.append(cols)
            for product, cols in zip(products, places):
                for h in range(2):
                    grad[cols[h]] = grad[cols[h]] + product[:, h * B : (h + 1) * B]

        each_pair(bounds_ref, group, body)


def shrunk(cur, grad, eta, thresh):
    moved = cur - eta * (grad * (1.0 / 128.0))
    return jnp.maximum(moved - thresh, 0.0) + jnp.minimum(moved + thresh, 0.0)


def chunk(ref, k):
    return ref.at[pl.ds(k * CHUNK, CHUNK)]


def first_kernel(codes, owner, bounds, bits, margins, w, far, cur_b, goal, buf, sems):
    nchunks = w.shape[0] // CHUNK
    for k in range(nchunks):
        pltpu.make_async_copy(chunk(w, k), chunk(buf, k), sems.at[k]).start()
    goal[...] = margins[...].T * 128.0

    def turn(k, carry):
        pltpu.make_async_copy(chunk(w, k), chunk(buf, k), sems.at[k]).wait()
        for u in range(CHUNK):
            j = k * CHUNK + u
            cur_b[j] = buf[j].T.astype(jnp.bfloat16)
        return carry

    lax.fori_loop(0, nchunks, turn, 0)
    forward(codes, owner, bounds, bits, cur_b, (FAR,), (far,))


def middle_kernel(
    codes, owner, bounds, step, pen, bits, e0, e1, e2, e3, w, far, cur_b, new, buf, grad, sem, sems
):
    nchunks = w.shape[0] // CHUNK
    load = pltpu.make_async_copy(w, buf, sem)
    load.start()
    backward(codes, owner, bounds, bits, (e0, e1, e2, e3), grad)
    load.wait()
    eta = step[0]
    thresh = eta * pen[0]

    def update(k, carry):
        for u in range(CHUNK):
            j = k * CHUNK + u
            block = shrunk(buf[j].T, grad[j], eta, thresh)
            grad[j] = block
            cur_b[j] = block.astype(jnp.bfloat16)
        pltpu.make_async_copy(chunk(grad, k), chunk(new, k), sems.at[k]).start()
        return carry

    lax.fori_loop(0, nchunks, update, 0)
    forward(codes, owner, bounds, bits, cur_b, (FAR,), (far,))
    for k in range(nchunks):
        pltpu.make_async_copy(chunk(grad, k), chunk(new, k), sems.at[k]).wait()


def near_kernel(codes, owner, bounds, bits, cur_b, p1, p3):
    forward(codes, owner, bounds, bits, cur_b, (1, 3), (p1, p3))


def own_kernel(codes, owner, bounds, bits, cur_b, p0):
    forward(codes, owner, bounds, bits, cur_b, (0,), (p0,))


def last_kernel(
    codes, owner, bounds, step, pen, bits, e0, e1, e2, e3, cur, out, buf, grad, sem, sems
):
    nchunks = cur.shape[0] // CHUNK
    load = pltpu.make_async_copy(cur, buf, sem)
    load.start()
    backward(codes, owner, bounds, bits, (e0, e1, e2, e3), grad)
    load.wait()
    eta = step[0]
    thresh = eta * pen[0]

    def update(k, carry):
        for u in range(CHUNK):
            j = k * CHUNK + u
            grad[j] = shrunk(buf[j], grad[j], eta, thresh).T
        pltpu.make_async_copy(chunk(grad, k), chunk(out, k), sems.at[k]).start()
        return carry

    lax.fori_loop(0, nchunks, update, 0)
    for k in range(nchunks):
        pltpu.make_async_copy(chunk(grad, k), chunk(out, k), sems.at[k]).wait()


def run_kernel(kernel, smem, vmem, hbm, outs, out_hbm, scratch, pairs):
    in_specs = [pl.BlockSpec(memory_space=pltpu.SMEM)] * len(smem)
    in_specs += [pl.BlockSpec(memory_space=pltpu.VMEM)] * len(vmem)
    in_specs += [pl.BlockSpec(memory_space=pltpu.HBM)] * len(hbm)
    out_specs = [pl.BlockSpec(memory_space=pltpu.VMEM)] * len(outs)
    out_specs += [pl.BlockSpec(memory_space=pltpu.HBM)] * len(out_hbm)
    return pl.pallas_call(
        kernel,
        out_shape=[jax.ShapeDtypeStruct(s, d) for s, d in (*outs, *out_hbm)],
        in_specs=in_specs,
        out_specs=out_specs,
        scratch_shapes=scratch,
        compiler_params=pltpu.CompilerParams(vmem_limit_bytes=(49 if hbm else 32) * MIB),
        cost_estimate=pl.CostEstimate(
            flops=pairs * 16 * B * B * B, bytes_accessed=4 * 1024 * 1024, transcendentals=0
        ),
    )(*smem, *vmem, *hbm)


def send_parts(lists, bits, cur_b, far):
    part = ((NZ, B, B), jnp.bfloat16)
    total = shift(far, 2, 0)
    one, three = run_kernel(near_kernel, lists, (bits, cur_b), (), [part] * 2, [], [], 80)
    up = shift(one, 1, 0)
    down = shift(three, 3, 0)
    (own,) = run_kernel(own_kernel, lists, (bits, cur_b), (), [part], [], [], 40)
    total = own.astype(jnp.float32) + total.astype(jnp.float32)
    return total + up.astype(jnp.float32) + down.astype(jnp.float32)


def reduce_runs(total, goal):
    low = total.astype(jnp.bfloat16)
    mine = total[0:2]
    for dz, at in ((2, 6), (1, 2), (7, 4)):
        mine = mine + shift(low[at : at + 2], 0, dz).astype(jnp.float32)
    mine = jnp.stack([mine[0] - goal, mine[1]])
    other = shift(jnp.flip(mine, 0).astype(jnp.bfloat16), 0, 4)
    return (mine + other.astype(jnp.float32)) * (1.0 / 128.0)


def gather_runs(two):
    eight = jnp.concatenate([two, shift(two, 0, 7), shift(two, 0, 1), shift(two, 0, 6)])
    return [eight, shift(eight, 3, 0), shift(eight, 2, 0), shift(eight, 1, 0)]


def per_device(weights_init, margins, block_bits, run, col, tally, step_size, penalty):
    nblocks = weights_init.shape[0] // B
    bits = block_bits.transpose(0, 2, 1)
    lists = build_lists(run, col, tally)
    weights = weights_init.reshape(nblocks, B, B)
    part = ((NZ, B, B), jnp.bfloat16)
    table = ((nblocks, B, B), jnp.float32)
    table_b = ((nblocks, B, B), jnp.bfloat16)
    buffer = pltpu.VMEM(*table)
    single = pltpu.SemaphoreType.DMA
    many = pltpu.SemaphoreType.DMA((nblocks // CHUNK,))

    far, cur_b, goal = run_kernel(
        first_kernel,
        lists,
        (bits, margins),
        (weights,),
        [part, table_b, ((B, B), jnp.float32)],
        [],
        [buffer, many],
        80,
    )
    err = reduce_runs(send_parts(lists, bits, cur_b, far), goal)
    errs = gather_runs(err.astype(jnp.bfloat16))
    far, cur_b, cur = run_kernel(
        middle_kernel,
        (*lists, step_size, penalty),
        (bits, *errs),
        (weights,),
        [part, table_b],
        [table],
        [buffer, buffer, single, many],
        240,
    )
    err = reduce_runs(send_parts(lists, bits, cur_b, far), goal)
    errs = gather_runs(err.astype(jnp.bfloat16))
    squares = jnp.sum(err[0] * err[0], axis=0)
    for hop in (1, 2, 4):
        squares = squares + lax.ppermute(squares, "tgt", [(k, k ^ hop) for k in range(8)])
    (out,) = run_kernel(
        last_kernel,
        (*lists, step_size, penalty),
        (bits, *errs),
        (cur,),
        [],
        [table],
        [buffer, buffer, single, many],
        200,
    )
    return out.reshape(weights_init.shape), squares / TARGETS


def solution(mesh):
    return jax.shard_map(
        per_device,
        mesh=mesh,
        in_specs=(
            P("clus", "tgt"),
            P("clus", "tgt"),
            P("clus", None, None),
            P("clus"),
            P("clus"),
            P("clus"),
            P(),
            P(),
        ),
        out_specs=(P("clus", "tgt"), P("clus")),
        check_vma=False,
    )
```

time: 1010 us -> 158 us (0.16)
  waiting for transfers between devices: 574 us -> 51.9 us
  matrix products: 309 us -> 0 us
  local copies, waits for them, and re-layouts: 59.1 us -> 2.26 us
  starting transfers between devices: 0.34 us -> 50.9 us
  Pallas kernels: 0 us -> 44 us
  other arithmetic: 36.5 us -> 4.63 us
  between operations: 15.9 us -> 3.02 us
  blocking collectives: 10.2 us -> 0 us
    reduce_scatter x2 -> x0, waiting for transfers between devices: 435 us -> none  [per_device(): lax.psum_scatter(total.reshape(ndev * BLOCK_ENTRIES, tcols).astype(jnp.bf...]
    dot_general x96 -> x0, matrix products: 309 us -> none  [the longest x32 211 us: add_blocks(): jnp.dot(selector, flat, preferred_element_type=jnp.float32, precision=lax...]
    all_gather x2 -> x0, waiting for transfers between devices: 139 us -> none  [per_device(): lax.all_gather(err_b, 'clus', axis=0, tiled=True)]
    ppermute x0 -> x29, waiting for transfers between devices: none -> 51.9 us  [the longest x26 44.8 us: shift(): return lax.ppermute(x, 'clus', pairs)]
    ppermute x0 -> x29, starting transfers between devices: none -> 50.9 us  [the longest x26 48.1 us: shift(): return lax.ppermute(x, 'clus', pairs)]
    pallas_call x0 -> x7, Pallas kernels: none -> 44 us  [run_kernel(): pl.pallas_call(kernel, out_shape=[jax.ShapeDtypeStruct(s, d) for s, d in...]
    mul x4 -> x0, other arithmetic: 25.3 us -> none  [the longest x1 14.9 us: per_device(): (2 * packed_flags - 1).astype(jnp.bfloat16)]
    unnamed x19 -> x6, local copies, waits for them, and re-layouts: 15.9 us -> 2.11 us
  transfers between devices with their start and end apart: 4 -> 29, of which waited for: 4 -> 23; matrix products, arithmetic and copies ran while one was open for 0% -> 0% of each run, Pallas kernels for 0% -> 4%
where the time goes in v1:
time: 158 us; the launch traced here: 157 us
  waiting for transfers between devices  51.9 us (33%)
  starting transfers between devices  50.9 us (32%)
  Pallas kernels  44 us (28%)
  other arithmetic  4.63 us (3%)
  between operations  3.02 us (2%)
  local copies, waits for them, and re-layouts  2.26 us (1%)
    ppermute x26, starting transfers between devices, shift(): return lax.ppermute(x, 'clus', pairs)  48.1 us
    ppermute x26, waiting for transfers between devices, shift(): return lax.ppermute(x, 'clus', pairs)  44.8 us
    pallas_call x7, Pallas kernels, run_kernel(): pl.pallas_call(kernel, out_shape=[jax.ShapeDtypeStruct(s, d) for s, d in...  44 us
    ppermute x3, waiting for transfers between devices, per_device(): lax.ppermute(squares, 'tgt', [(k, k ^ hop) for k in range(8)])  7.07 us
  transfers between devices with their start and end apart: 29, of which 23 were waited for; matrix products, arithmetic and copies ran while one was open for 0% of the time, Pallas kernels for 4%

profile of v1, /device:TPU:2, one launch (start us, length us, event | category | flops | bytes accessed | tf_op | source)
XLA Modules:
  0.0 156.7 jit_solution(11418266831974474536)
XLA Ops:
  1.3 0.7 fusion.14
  2.0 0.1 convert_reduce_fusion.1
  2.1 0.6 fusion.21
  3.1 0.2 convert_reduce_fusion
  3.4 0.7 pad_add_fusion.bounds
  4.1 0.7 add_add_fusion
  4.8 0.2 select_reduce_fusion.codes
  5.0 1.3 copy-done
  6.2 0.8 copy-done.2
  7.1 5.2 %shard_map.95 = (bf16[8,128,128]{2,1,0:T(8,128)(2,1)S(1)}, bf16[64,128,128]{2,1,0:T(8,128)(2,1)S(1)}, f32[128,128]{1,0:T(8,128)S(1)}) custom-call(s32[328]{0:T(512)S(1)} %select_reduce_fusion.codes, s32[164]{0:T(256)S(1)} %broadcast_minimum_fusion.owner, s32[5]{0:T(128)S(1)} %pad_add_fusion.bounds, s32[288,8,128]{2,1,0:T(8,128)S(1)} %bitcast.23, ...), custom_call_target="tpu_custom_call" | custom-call | flops 2684354560 | bytes 4194304 | tf_op jit(solution)/shard_map/pallas_call | solution.py:237
  12.2 4.4 %shard_map.97 = (bf16[8,128,128]{2,1,0:T(8,128)(2,1)S(1)}, bf16[8,128,128]{2,1,0:T(8,128)(2,1)S(1)}) custom-call(s32[328]{0:T(512)S(1)} %select_reduce_fusion.codes, s32[164]{0:T(256)S(1)} %broadcast_minimum_fusion.owner, s32[5]{0:T(128)S(1)} %pad_add_fusion.bounds, s32[288,8,128]{2,1,0:T(8,128)S(1)} %bitcast.24, ...), custom_call_target="tpu_custom_call" | custom-call | flops 2684354560 | bytes 4194304 | tf_op jit(solution)/shard_map/pallas_call | solution.py:237
  16.7 1.1 collective-permute-start.1
  17.8 3.9 %collective-permute-start.2 = (bf16[8,128,128]{2,1,0:T(8,128)(2,1)S(1)}, bf16[8,128,128]{2,1,0:T(8,128)(2,1)S(1)}, u32[]{:S(2)}, u32[]{:S(2)}) collective-permute-start(bf16[8,128,128]{2,1,0:T(8,128)(2,1)S(1)} %get-tuple-element.15), channel_id=1, source_target_pairs={{0,192},{8,200},{16,208},{24,216},{32,224},{40,232},{48,240},{56,2... | collective-permute-start | bytes 786440 | tf_op jit(solution)/shard_map/ppermute | solution.py:28
  21.7 1.4 collective-permute-start
  23.1 2.8 %shard_map.96 = bf16[8,128,128]{2,1,0:T(8,128)(2,1)S(1)} custom-call(s32[328]{0:T(512)S(1)} %select_reduce_fusion.codes, s32[164]{0:T(256)S(1)} %broadcast_minimum_fusion.owner, s32[5]{0:T(128)S(1)} %pad_add_fusion.bounds, s32[288,8,128]{2,1,0:T(8,128)S(1)} %bitcast.25, bf16[64,128,128]{2,1,0:T(8,128)(2,1)S(1)} %get-tuple-element.12.cur_b), custom_call_target="tpu_custom_call" | custom-call | flops 1342177280 | bytes 4194304 | tf_op jit(solution)/shard_map/pallas_call | solution.py:237
  25.9 2.0 %collective-permute-done.1 = bf16[8,128,128]{2,1,0:T(8,128)(2,1)S(1)} collective-permute-done((bf16[8,128,128]{2,1,0:T(8,128)(2,1)S(1)}, bf16[8,128,128]{2,1,0:T(8,128)(2,1)S(1)}, u32[]{:S(2)}, u32[]{:S(2)}) %collective-permute-start.1) | collective-permute-done | bytes 262176 | tf_op jit(solution)/shard_map/ppermute | solution.py:28
  28.0 5.0 %collective-permute-done.2 = bf16[8,128,128]{2,1,0:T(8,128)(2,1)S(1)} collective-permute-done((bf16[8,128,128]{2,1,0:T(8,128)(2,1)S(1)}, bf16[8,128,128]{2,1,0:T(8,128)(2,1)S(1)}, u32[]{:S(2)}, u32[]{:S(2)}) %collective-permute-start.2) | collective-permute-done | bytes 262176 | tf_op jit(solution)/shard_map/ppermute | solution.py:28
  32.9 1.8 %collective-permute-done = bf16[8,128,128]{2,1,0:T(8,128)(2,1)S(1)} collective-permute-done((bf16[8,128,128]{2,1,0:T(8,128)(2,1)S(1)}, bf16[8,128,128]{2,1,0:T(8,128)(2,1)S(1)}, u32[]{:S(2)}, u32[]{:S(2)}) %collective-permute-start) | collective-permute-done | bytes 262176 | tf_op jit(solution)/shard_map/ppermute | solution.py:28
  34.8 0.1 fusion.20
  34.9 0.4 collective-permute-start.3
  35.3 4.8 %collective-permute-start.5 = (bf16[2,128,128]{2,1,0:T(8,128)(2,1)S(1)}, bf16[2,128,128]{2,1,0:T(8,128)(2,1)S(1)}, u32[]{:S(2)}, u32[]{:S(2)}) collective-permute-start(bf16[2,128,128]{2,1,0:T(8,128)(2,1)S(1)} %get-tuple-element.34), channel_id=1, source_target_pairs={{0,56},{8,0},{16,8},{24,16},{32,24},{40,32},{48,40},{56,48},{64,12... | collective-permute-start | bytes 196616 | tf_op jit(solution)/shard_map/ppermute | solution.py:28
  40.1 0.3 collective-permute-start.4
  40.5 3.4 %collective-permute-done.3 = bf16[2,128,128]{2,1,0:T(8,128)(2,1)S(1)} collective-permute-done((bf16[2,128,128]{2,1,0:T(8,128)(2,1)S(1)}, bf16[2,128,128]{2,1,0:T(8,128)(2,1)S(1)}, u32[]{:S(2)}, u32[]{:S(2)}) %collective-permute-start.3) | collective-permute-done | bytes 65568 | tf_op jit(solution)/shard_map/ppermute | solution.py:28
  43.9 1.8 %collective-permute-done.4 = bf16[2,128,128]{2,1,0:T(8,128)(2,1)S(1)} collective-permute-done((bf16[2,128,128]{2,1,0:T(8,128)(2,1)S(1)}, bf16[2,128,128]{2,1,0:T(8,128)(2,1)S(1)}, u32[]{:S(2)}, u32[]{:S(2)}) %collective-permute-start.4) | collective-permute-done | bytes 65568 | tf_op jit(solution)/shard_map/ppermute | solution.py:28
  45.7 4.5 %collective-permute-start.6 = (bf16[2,128,128]{2,1,0:T(8,128)(2,1)S(1)}, bf16[2,128,128]{2,1,0:T(8,128)(2,1)S(1)}, u32[]{:S(2)}, u32[]{:S(2)}) collective-permute-start(bf16[2,128,128]{2,1,0:T(8,128)(2,1)S(1)} %rev.12), channel_id=1, source_target_pairs={{0,32},{8,40},{16,48},{24,56},{32,0},{40,8},{48,16},{56,24},{64,96... | collective-permute-start | bytes 196616 | tf_op jit(solution)/shard_map/ppermute | solution.py:28
  50.2 3.8 %collective-permute-done.6 = bf16[2,128,128]{2,1,0:T(8,128)(2,1)S(1)} collective-permute-done((bf16[2,128,128]{2,1,0:T(8,128)(2,1)S(1)}, bf16[2,128,128]{2,1,0:T(8,128)(2,1)S(1)}, u32[]{:S(2)}, u32[]{:S(2)}) %collective-permute-start.6) | collective-permute-done | bytes 65568 | tf_op jit(solution)/shard_map/ppermute | solution.py:28
  54.0 1.4 collective-permute-start.9
  55.4 0.2 collective-permute-start.8
  55.6 3.0 %collective-permute-start.7 = (bf16[2,128,128]{2,1,0:T(8,128)(2,1)S(1)}, bf16[2,128,128]{2,1,0:T(8,128)(2,1)S(1)}, u32[]{:S(2)}, u32[]{:S(2)}) collective-permute-start(bf16[2,128,128]{2,1,0:T(8,128)(2,1)S(1)} %multiply_convert_fusion), channel_id=1, source_target_pairs={{0,56},{8,0},{16,8},{24,16},{32,24},{40,32},{48,40},{56,48},{64,12... | collective-permute-start | bytes 196616 | tf_op jit(solution)/shard_map/ppermute | solution.py:28
  58.6 0.9 collective-permute-done.9
  59.5 1.3 collective-permute-done.8
  60.9 1.7 %collective-permute-start.12 = (bf16[8,128,128]{2,1,0:T(8,128)(2,1)S(1)}, bf16[8,128,128]{2,1,0:T(8,128)(2,1)S(1)}, u32[]{:S(2)}, u32[]{:S(2)}) collective-permute-start(bf16[8,128,128]{2,1,0:T(8,128)(2,1)S(1)} %pad_maximum_fusion.e0), channel_id=1, source_target_pairs={{0,64},{8,72},{16,80},{24,88},{32,96},{40,104},{48,112},{56,120},{... | collective-permute-start | bytes 786440 | tf_op jit(solution)/shard_map/ppermute | solution.py:28
  62.6 2.6 %collective-permute-start.11 = (bf16[8,128,128]{2,1,0:T(8,128)(2,1)S(1)}, bf16[8,128,128]{2,1,0:T(8,128)(2,1)S(1)}, u32[]{:S(2)}, u32[]{:S(2)}) collective-permute-start(bf16[8,128,128]{2,1,0:T(8,128)(2,1)S(1)} %pad_maximum_fusion.e0), channel_id=1, source_target_pairs={{0,128},{8,136},{16,144},{24,152},{32,160},{40,168},{48,176},{56,1... | collective-permute-start | bytes 786440 | tf_op jit(solution)/shard_map/ppermute | solution.py:28
  65.1 0.2 collective-permute-start.10
  66.6 2.5 %collective-permute-done.12.e3 = bf16[8,128,128]{2,1,0:T(8,128)(2,1)S(1)} collective-permute-done((bf16[8,128,128]{2,1,0:T(8,128)(2,1)S(1)}, bf16[8,128,128]{2,1,0:T(8,128)(2,1)S(1)}, u32[]{:S(2)}, u32[]{:S(2)}) %collective-permute-start.12) | collective-permute-done | bytes 262176 | tf_op jit(solution)/shard_map/ppermute | solution.py:28
  69.1 3.2 %collective-permute-done.11.e2 = bf16[8,128,128]{2,1,0:T(8,128)(2,1)S(1)} collective-permute-done((bf16[8,128,128]{2,1,0:T(8,128)(2,1)S(1)}, bf16[8,128,128]{2,1,0:T(8,128)(2,1)S(1)}, u32[]{:S(2)}, u32[]{:S(2)}) %collective-permute-start.11) | collective-permute-done | bytes 262176 | tf_op jit(solution)/shard_map/ppermute | solution.py:28
  72.4 13.0 %shard_map.98 = (bf16[8,128,128]{2,1,0:T(8,128)(2,1)S(1)}, bf16[64,128,128]{2,1,0:T(8,128)(2,1)S(1)}, f32[64,128,128]{2,1,0:T(8,128)}) custom-call(s32[328]{0:T(512)S(1)} %select_reduce_fusion.codes, s32[164]{0:T(256)S(1)} %broadcast_minimum_fusion.owner, s32[5]{0:T(128)S(1)} %pad_add_fusion.bounds, f32[1]{0:T(128)S(6)} %copy.11.step, f32[1]{0:T(128)S(6)} %copy.12.pen, ...), custom_call_target="tpu_custom_call" | custom-call | flops 8053063680 | bytes 4194304 | tf_op jit(solution)/shard_map/pallas_call | solution.py:237
  85.4 4.4 %shard_map.100 = (bf16[8,128,128]{2,1,0:T(8,128)(2,1)S(1)}, bf16[8,128,128]{2,1,0:T(8,128)(2,1)S(1)}) custom-call(s32[328]{0:T(512)S(1)} %select_reduce_fusion.codes, s32[164]{0:T(256)S(1)} %broadcast_minimum_fusion.owner, s32[5]{0:T(128)S(1)} %pad_add_fusion.bounds, s32[288,8,128]{2,1,0:T(8,128)S(1)} %bitcast.27, ...), custom_call_target="tpu_custom_call" | custom-call | flops 2684354560 | bytes 4194304 | tf_op jit(solution)/shard_map/pallas_call | solution.py:237
  90.0 6.7 %collective-permute-start.15 = (bf16[8,128,128]{2,1,0:T(8,128)(2,1)S(1)}, bf16[8,128,128]{2,1,0:T(8,128)(2,1)S(1)}, u32[]{:S(2)}, u32[]{:S(2)}) collective-permute-start(bf16[8,128,128]{2,1,0:T(8,128)(2,1)S(1)} %get-tuple-element.20), channel_id=1, source_target_pairs={{0,192},{8,200},{16,208},{24,216},{32,224},{40,232},{48,240},{56,2... | collective-permute-start | bytes 786440 | tf_op jit(solution)/shard_map/ppermute | solution.py:28
  96.7 1.4 collective-permute-start.13
  98.0 2.8 %shard_map.99 = bf16[8,128,128]{2,1,0:T(8,128)(2,1)S(1)} custom-call(s32[328]{0:T(512)S(1)} %select_reduce_fusion.codes, s32[164]{0:T(256)S(1)} %broadcast_minimum_fusion.owner, s32[5]{0:T(128)S(1)} %pad_add_fusion.bounds, s32[288,8,128]{2,1,0:T(8,128)S(1)} %bitcast.28, bf16[64,128,128]{2,1,0:T(8,128)(2,1)S(1)} %get-tuple-element.17.cur_b), custom_call_target="tpu_custom_call" | custom-call | flops 1342177280 | bytes 4194304 | tf_op jit(solution)/shard_map/pallas_call | solution.py:237
  100.8 0.7 collective-permute-done.14
  101.5 2.3 %collective-permute-done.15 = bf16[8,128,128]{2,1,0:T(8,128)(2,1)S(1)} collective-permute-done((bf16[8,128,128]{2,1,0:T(8,128)(2,1)S(1)}, bf16[8,128,128]{2,1,0:T(8,128)(2,1)S(1)}, u32[]{:S(2)}, u32[]{:S(2)}) %collective-permute-start.15) | collective-permute-done | bytes 262176 | tf_op jit(solution)/shard_map/ppermute | solution.py:28
  103.8 1.4 collective-permute-done.13
  105.2 0.1 fusion.19
  105.5 4.7 %collective-permute-start.18 = (bf16[2,128,128]{2,1,0:T(8,128)(2,1)S(1)}, bf16[2,128,128]{2,1,0:T(8,128)(2,1)S(1)}, u32[]{:S(2)}, u32[]{:S(2)}) collective-permute-start(bf16[2,128,128]{2,1,0:T(8,128)(2,1)S(1)} %get-tuple-element.31), channel_id=1, source_target_pairs={{0,56},{8,0},{16,8},{24,16},{32,24},{40,32},{48,40},{56,48},{64,12... | collective-permute-start | bytes 196616 | tf_op jit(solution)/shard_map/ppermute | solution.py:28
  110.2 1.6 %collective-permute-done.16 = bf16[2,128,128]{2,1,0:T(8,128)(2,1)S(1)} collective-permute-done((bf16[2,128,128]{2,1,0:T(8,128)(2,1)S(1)}, bf16[2,128,128]{2,1,0:T(8,128)(2,1)S(1)}, u32[]{:S(2)}, u32[]{:S(2)}) %collective-permute-start.16) | collective-permute-done | bytes 65568 | tf_op jit(solution)/shard_map/ppermute | solution.py:28
  111.8 1.1 collective-permute-done.18
  112.9 3.3 %collective-permute-done.17 = bf16[2,128,128]{2,1,0:T(8,128)(2,1)S(1)} collective-permute-done((bf16[2,128,128]{2,1,0:T(8,128)(2,1)S(1)}, bf16[2,128,128]{2,1,0:T(8,128)(2,1)S(1)}, u32[]{:S(2)}, u32[]{:S(2)}) %collective-permute-start.17) | collective-permute-done | bytes 65568 | tf_op jit(solution)/shard_map/ppermute | solution.py:28
  116.3 2.4 %collective-permute-start.19 = (bf16[2,128,128]{2,1,0:T(8,128)(2,1)S(1)}, bf16[2,128,128]{2,1,0:T(8,128)(2,1)S(1)}, u32[]{:S(2)}, u32[]{:S(2)}) collective-permute-start(bf16[2,128,128]{2,1,0:T(8,128)(2,1)S(1)} %rev.11), channel_id=1, source_target_pairs={{0,32},{8,40},{16,48},{24,56},{32,0},{40,8},{48,16},{56,24},{64,96... | collective-permute-start | bytes 196616 | tf_op jit(solution)/shard_map/ppermute | solution.py:28
  118.7 5.8 %collective-permute-done.19 = bf16[2,128,128]{2,1,0:T(8,128)(2,1)S(1)} collective-permute-done((bf16[2,128,128]{2,1,0:T(8,128)(2,1)S(1)}, bf16[2,128,128]{2,1,0:T(8,128)(2,1)S(1)}, u32[]{:S(2)}, u32[]{:S(2)}) %collective-permute-start.19) | collective-permute-done | bytes 65568 | tf_op jit(solution)/shard_map/ppermute | solution.py:28
  124.7 1.7 %collective-permute-start.21 = (bf16[2,128,128]{2,1,0:T(8,128)(2,1)S(1)}, bf16[2,128,128]{2,1,0:T(8,128)(2,1)S(1)}, u32[]{:S(2)}, u32[]{:S(2)}) collective-permute-start(bf16[2,128,128]{2,1,0:T(8,128)(2,1)S(1)} %get-tuple-element.22), channel_id=1, source_target_pairs={{0,8},{8,16},{16,24},{24,32},{32,40},{40,48},{48,56},{56,0},{64,72... | collective-permute-start | bytes 196616 | tf_op jit(solution)/shard_map/ppermute | solution.py:28
  126.4 1.6 %collective-permute-start.20 = (bf16[2,128,128]{2,1,0:T(8,128)(2,1)S(1)}, bf16[2,128,128]{2,1,0:T(8,128)(2,1)S(1)}, u32[]{:S(2)}, u32[]{:S(2)}) collective-permute-start(bf16[2,128,128]{2,1,0:T(8,128)(2,1)S(1)} %get-tuple-element.22), channel_id=1, source_target_pairs={{0,56},{8,0},{16,8},{24,16},{32,24},{40,32},{48,40},{56,48},{64,12... | collective-permute-start | bytes 196616 | tf_op jit(solution)/shard_map/ppermute | solution.py:28
  128.0 2.4 %collective-permute-done.22 = bf16[2,128,128]{2,1,0:T(8,128)(2,1)S(1)} collective-permute-done((bf16[2,128,128]{2,1,0:T(8,128)(2,1)S(1)}, bf16[2,128,128]{2,1,0:T(8,128)(2,1)S(1)}, u32[]{:S(2)}, u32[]{:S(2)}) %collective-permute-start.22) | collective-permute-done | bytes 65568 | tf_op jit(solution)/shard_map/ppermute | solution.py:28
  130.4 0.5 collective-permute-done.20
  130.9 0.8 collective-permute-start.25
  131.7 3.0 %collective-permute-start.24 = (bf16[8,128,128]{2,1,0:T(8,128)(2,1)S(1)}, bf16[8,128,128]{2,1,0:T(8,128)(2,1)S(1)}, u32[]{:S(2)}, u32[]{:S(2)}) collective-permute-start(bf16[8,128,128]{2,1,0:T(8,128)(2,1)S(1)} %pad_maximum_fusion.1.e0), channel_id=1, source_target_pairs={{0,128},{8,136},{16,144},{24,152},{32,160},{40,168},{48,176},{56,1... | collective-permute-start | bytes 786440 | tf_op jit(solution)/shard_map/ppermute | solution.py:28
  134.9 1.1 collective-permute-done.26
  136.0 0.6 collective-permute-start.27
  136.6 3.0 %collective-permute-done.27 = f32[128]{0:T(128)S(1)} collective-permute-done((f32[128]{0:T(128)S(1)}, f32[128]{0:T(128)S(1)}, u32[]{:S(2)}, u32[]{:S(2)}) %collective-permute-start.27) | collective-permute-done | bytes 544 | tf_op jit(solution)/shard_map/ppermute | solution.py:314
  139.6 2.2 %collective-permute-start.28 = (f32[128]{0:T(128)S(1)}, f32[128]{0:T(128)S(1)}, u32[]{:S(2)}, u32[]{:S(2)}) collective-permute-start(f32[128]{0:T(128)S(1)} %add.170), channel_id=1, source_target_pairs={{0,4},{1,5},{2,6},{3,7},{4,0},{5,1},{6,2},{7,3},{8,12},{9,13},{10,... | collective-permute-start | bytes 1544 | tf_op jit(solution)/shard_map/ppermute | solution.py:314
  141.8 2.9 %collective-permute-done.28 = f32[128]{0:T(128)S(1)} collective-permute-done((f32[128]{0:T(128)S(1)}, f32[128]{0:T(128)S(1)}, u32[]{:S(2)}, u32[]{:S(2)}) %collective-permute-start.28) | collective-permute-done | bytes 544 | tf_op jit(solution)/shard_map/ppermute | solution.py:314
  144.7 0.5 add_multiply_fusion.1
  145.2 11.4 %shard_map.101 = f32[64,128,128]{2,1,0:T(8,128)} custom-call(s32[328]{0:T(512)S(1)} %select_reduce_fusion.codes, s32[164]{0:T(256)S(1)} %broadcast_minimum_fusion.owner, s32[5]{0:T(128)S(1)} %pad_add_fusion.bounds, f32[1]{0:T(128)S(6)} %copy.11.step, f32[1]{0:T(128)S(6)} %copy.12.pen, s32[288,8,128]{2,1,0:T(8,128)S(1)} %bitcast.29, ...), custom_call_target="tpu_custom_call" | custom-call | flops 6710886400 | bytes 4194304 | tf_op jit(solution)/shard_map/pallas_call | solution.py:237
  (42 shorter events, 1.3 us)
Async XLA Ops:
  5.0 1.3 copy-start
  6.2 0.8 copy-start.2
  16.7 11.3 %collective-permute-start.1 = (bf16[8,128,128]{2,1,0:T(8,128)(2,1)S(1)}, bf16[8,128,128]{2,1,0:T(8,128)(2,1)S(1)}, u32[]{:S(2)}, u32[]{:S(2)}) collective-permute-start(bf16[8,128,128]{2,1,0:T(8,128)(2,1)S(1)} %get-tuple-element.14), channel_id=1, source_target_pairs={{0,64},{8,72},{16,80},{24,88},{32,96},{40,104},{48,112},{56,120},{... | collective-permute-start | bytes 786440 | tf_op jit(solution)/shard_map/ppermute | solution.py:28
  17.8 15.1 %collective-permute-start.2 = (bf16[8,128,128]{2,1,0:T(8,128)(2,1)S(1)}, bf16[8,128,128]{2,1,0:T(8,128)(2,1)S(1)}, u32[]{:S(2)}, u32[]{:S(2)}) collective-permute-start(bf16[8,128,128]{2,1,0:T(8,128)(2,1)S(1)} %get-tuple-element.15), channel_id=1, source_target_pairs={{0,192},{8,200},{16,208},{24,216},{32,224},{40,232},{48,240},{56,2... | collective-permute-start | bytes 786440 | tf_op jit(solution)/shard_map/ppermute | solution.py:28
  21.7 50.6 %copy-start.1 = (s32[288,128,8]{1,2,0:T(8,128)S(1)}, s32[288,128,8]{1,2,0:T(8,128)}, u32[]{:S(2)}) copy-start(s32[288,128,8]{1,2,0:T(8,128)} %param.10) | copy-start | bytes 3538948
  21.7 13.0 %collective-permute-start = (bf16[8,128,128]{2,1,0:T(8,128)(2,1)S(1)}, bf16[8,128,128]{2,1,0:T(8,128)(2,1)S(1)}, u32[]{:S(2)}, u32[]{:S(2)}) collective-permute-start(bf16[8,128,128]{2,1,0:T(8,128)(2,1)S(1)} %get-tuple-element.13), channel_id=1, source_target_pairs={{0,128},{8,136},{16,144},{24,152},{32,160},{40,168},{48,176},{56,1... | collective-permute-start | bytes 786440 | tf_op jit(solution)/shard_map/ppermute | solution.py:28
  34.9 8.9 %collective-permute-start.3 = (bf16[2,128,128]{2,1,0:T(8,128)(2,1)S(1)}, bf16[2,128,128]{2,1,0:T(8,128)(2,1)S(1)}, u32[]{:S(2)}, u32[]{:S(2)}) collective-permute-start(bf16[2,128,128]{2,1,0:T(8,128)(2,1)S(1)} %get-tuple-element.33), channel_id=1, source_target_pairs={{0,16},{8,24},{16,32},{24,40},{32,48},{40,56},{48,0},{56,8},{64,80... | collective-permute-start | bytes 196616 | tf_op jit(solution)/shard_map/ppermute | solution.py:28
  35.3 8.5 %collective-permute-start.5 = (bf16[2,128,128]{2,1,0:T(8,128)(2,1)S(1)}, bf16[2,128,128]{2,1,0:T(8,128)(2,1)S(1)}, u32[]{:S(2)}, u32[]{:S(2)}) collective-permute-start(bf16[2,128,128]{2,1,0:T(8,128)(2,1)S(1)} %get-tuple-element.34), channel_id=1, source_target_pairs={{0,56},{8,0},{16,8},{24,16},{32,24},{40,32},{48,40},{56,48},{64,12... | collective-permute-start | bytes 196616 | tf_op jit(solution)/shard_map/ppermute | solution.py:28
  40.1 5.5 %collective-permute-start.4 = (bf16[2,128,128]{2,1,0:T(8,128)(2,1)S(1)}, bf16[2,128,128]{2,1,0:T(8,128)(2,1)S(1)}, u32[]{:S(2)}, u32[]{:S(2)}) collective-permute-start(bf16[2,128,128]{2,1,0:T(8,128)(2,1)S(1)} %get-tuple-element.35), channel_id=1, source_target_pairs={{0,8},{8,16},{16,24},{24,32},{32,40},{40,48},{48,56},{56,0},{64,72... | collective-permute-start | bytes 196616 | tf_op jit(solution)/shard_map/ppermute | solution.py:28
  45.7 8.3 %collective-permute-start.6 = (bf16[2,128,128]{2,1,0:T(8,128)(2,1)S(1)}, bf16[2,128,128]{2,1,0:T(8,128)(2,1)S(1)}, u32[]{:S(2)}, u32[]{:S(2)}) collective-permute-start(bf16[2,128,128]{2,1,0:T(8,128)(2,1)S(1)} %rev.12), channel_id=1, source_target_pairs={{0,32},{8,40},{16,48},{24,56},{32,0},{40,8},{48,16},{56,24},{64,96... | collective-permute-start | bytes 196616 | tf_op jit(solution)/shard_map/ppermute | solution.py:28
  54.0 5.5 %collective-permute-start.9 = (bf16[2,128,128]{2,1,0:T(8,128)(2,1)S(1)}, bf16[2,128,128]{2,1,0:T(8,128)(2,1)S(1)}, u32[]{:S(2)}, u32[]{:S(2)}) collective-permute-start(bf16[2,128,128]{2,1,0:T(8,128)(2,1)S(1)} %multiply_convert_fusion), channel_id=1, source_target_pairs={{0,48},{8,56},{16,0},{24,8},{32,16},{40,24},{48,32},{56,40},{64,11... | collective-permute-start | bytes 196616 | tf_op jit(solution)/shard_map/ppermute | solution.py:28
  55.4 5.5 %collective-permute-start.8 = (bf16[2,128,128]{2,1,0:T(8,128)(2,1)S(1)}, bf16[2,128,128]{2,1,0:T(8,128)(2,1)S(1)}, u32[]{:S(2)}, u32[]{:S(2)}) collective-permute-start(bf16[2,128,128]{2,1,0:T(8,128)(2,1)S(1)} %multiply_convert_fusion), channel_id=1, source_target_pairs={{0,8},{8,16},{16,24},{24,32},{32,40},{40,48},{48,56},{56,0},{64,72... | collective-permute-start | bytes 196616 | tf_op jit(solution)/shard_map/ppermute | solution.py:28
  55.6 5.3 %collective-permute-start.7 = (bf16[2,128,128]{2,1,0:T(8,128)(2,1)S(1)}, bf16[2,128,128]{2,1,0:T(8,128)(2,1)S(1)}, u32[]{:S(2)}, u32[]{:S(2)}) collective-permute-start(bf16[2,128,128]{2,1,0:T(8,128)(2,1)S(1)} %multiply_convert_fusion), channel_id=1, source_target_pairs={{0,56},{8,0},{16,8},{24,16},{32,24},{40,32},{48,40},{56,48},{64,12... | collective-permute-start | bytes 196616 | tf_op jit(solution)/shard_map/ppermute | solution.py:28
  60.9 8.2 %collective-permute-start.12 = (bf16[8,128,128]{2,1,0:T(8,128)(2,1)S(1)}, bf16[8,128,128]{2,1,0:T(8,128)(2,1)S(1)}, u32[]{:S(2)}, u32[]{:S(2)}) collective-permute-start(bf16[8,128,128]{2,1,0:T(8,128)(2,1)S(1)} %pad_maximum_fusion.e0), channel_id=1, source_target_pairs={{0,64},{8,72},{16,80},{24,88},{32,96},{40,104},{48,112},{56,120},{... | collective-permute-start | bytes 786440 | tf_op jit(solution)/shard_map/ppermute | solution.py:28
  62.6 9.7 %collective-permute-start.11 = (bf16[8,128,128]{2,1,0:T(8,128)(2,1)S(1)}, bf16[8,128,128]{2,1,0:T(8,128)(2,1)S(1)}, u32[]{:S(2)}, u32[]{:S(2)}) collective-permute-start(bf16[8,128,128]{2,1,0:T(8,128)(2,1)S(1)} %pad_maximum_fusion.e0), channel_id=1, source_target_pairs={{0,128},{8,136},{16,144},{24,152},{32,160},{40,168},{48,176},{56,1... | collective-permute-start | bytes 786440 | tf_op jit(solution)/shard_map/ppermute | solution.py:28
  65.1 7.3 %collective-permute-start.10 = (bf16[8,128,128]{2,1,0:T(8,128)(2,1)S(1)}, bf16[8,128,128]{2,1,0:T(8,128)(2,1)S(1)}, u32[]{:S(2)}, u32[]{:S(2)}) collective-permute-start(bf16[8,128,128]{2,1,0:T(8,128)(2,1)S(1)} %pad_maximum_fusion.e0), channel_id=1, source_target_pairs={{0,192},{8,200},{16,208},{24,216},{32,224},{40,232},{48,240},{56,2... | collective-permute-start | bytes 786440 | tf_op jit(solution)/shard_map/ppermute | solution.py:28
  89.9 11.7 %collective-permute-start.14 = (bf16[8,128,128]{2,1,0:T(8,128)(2,1)S(1)}, bf16[8,128,128]{2,1,0:T(8,128)(2,1)S(1)}, u32[]{:S(2)}, u32[]{:S(2)}) collective-permute-start(bf16[8,128,128]{2,1,0:T(8,128)(2,1)S(1)} %get-tuple-element.19), channel_id=1, source_target_pairs={{0,64},{8,72},{16,80},{24,88},{32,96},{40,104},{48,112},{56,120},{... | collective-permute-start | bytes 786440 | tf_op jit(solution)/shard_map/ppermute | solution.py:28
  90.0 13.8 %collective-permute-start.15 = (bf16[8,128,128]{2,1,0:T(8,128)(2,1)S(1)}, bf16[8,128,128]{2,1,0:T(8,128)(2,1)S(1)}, u32[]{:S(2)}, u32[]{:S(2)}) collective-permute-start(bf16[8,128,128]{2,1,0:T(8,128)(2,1)S(1)} %get-tuple-element.20), channel_id=1, source_target_pairs={{0,192},{8,200},{16,208},{24,216},{32,224},{40,232},{48,240},{56,2... | collective-permute-start | bytes 786440 | tf_op jit(solution)/shard_map/ppermute | solution.py:28
  96.7 8.5 %collective-permute-start.13 = (bf16[8,128,128]{2,1,0:T(8,128)(2,1)S(1)}, bf16[8,128,128]{2,1,0:T(8,128)(2,1)S(1)}, u32[]{:S(2)}, u32[]{:S(2)}) collective-permute-start(bf16[8,128,128]{2,1,0:T(8,128)(2,1)S(1)} %get-tuple-element.18), channel_id=1, source_target_pairs={{0,128},{8,136},{16,144},{24,152},{32,160},{40,168},{48,176},{56,1... | collective-permute-start | bytes 786440 | tf_op jit(solution)/shard_map/ppermute | solution.py:28
  105.4 6.5 %collective-permute-start.16 = (bf16[2,128,128]{2,1,0:T(8,128)(2,1)S(1)}, bf16[2,128,128]{2,1,0:T(8,128)(2,1)S(1)}, u32[]{:S(2)}, u32[]{:S(2)}) collective-permute-start(bf16[2,128,128]{2,1,0:T(8,128)(2,1)S(1)} %get-tuple-element.30), channel_id=1, source_target_pairs={{0,16},{8,24},{16,32},{24,40},{32,48},{40,56},{48,0},{56,8},{64,80... | collective-permute-start | bytes 196616 | tf_op jit(solution)/shard_map/ppermute | solution.py:28
  105.5 7.4 %collective-permute-start.18 = (bf16[2,128,128]{2,1,0:T(8,128)(2,1)S(1)}, bf16[2,128,128]{2,1,0:T(8,128)(2,1)S(1)}, u32[]{:S(2)}, u32[]{:S(2)}) collective-permute-start(bf16[2,128,128]{2,1,0:T(8,128)(2,1)S(1)} %get-tuple-element.31), channel_id=1, source_target_pairs={{0,56},{8,0},{16,8},{24,16},{32,24},{40,32},{48,40},{56,48},{64,12... | collective-permute-start | bytes 196616 | tf_op jit(solution)/shard_map/ppermute | solution.py:28
  110.1 6.1 %collective-permute-start.17 = (bf16[2,128,128]{2,1,0:T(8,128)(2,1)S(1)}, bf16[2,128,128]{2,1,0:T(8,128)(2,1)S(1)}, u32[]{:S(2)}, u32[]{:S(2)}) collective-permute-start(bf16[2,128,128]{2,1,0:T(8,128)(2,1)S(1)} %get-tuple-element.32), channel_id=1, source_target_pairs={{0,8},{8,16},{16,24},{24,32},{32,40},{40,48},{48,56},{56,0},{64,72... | collective-permute-start | bytes 196616 | tf_op jit(solution)/shard_map/ppermute | solution.py:28
  116.3 8.3 %collective-permute-start.19 = (bf16[2,128,128]{2,1,0:T(8,128)(2,1)S(1)}, bf16[2,128,128]{2,1,0:T(8,128)(2,1)S(1)}, u32[]{:S(2)}, u32[]{:S(2)}) collective-permute-start(bf16[2,128,128]{2,1,0:T(8,128)(2,1)S(1)} %rev.11), channel_id=1, source_target_pairs={{0,32},{8,40},{16,48},{24,56},{32,0},{40,8},{48,16},{56,24},{64,96... | collective-permute-start | bytes 196616 | tf_op jit(solution)/shard_map/ppermute | solution.py:28
  124.6 5.8 %collective-permute-start.22 = (bf16[2,128,128]{2,1,0:T(8,128)(2,1)S(1)}, bf16[2,128,128]{2,1,0:T(8,128)(2,1)S(1)}, u32[]{:S(2)}, u32[]{:S(2)}) collective-permute-start(bf16[2,128,128]{2,1,0:T(8,128)(2,1)S(1)} %get-tuple-element.22), channel_id=1, source_target_pairs={{0,48},{8,56},{16,0},{24,8},{32,16},{40,24},{48,32},{56,40},{64,11... | collective-permute-start | bytes 196616 | tf_op jit(solution)/shard_map/ppermute | solution.py:28
  124.7 5.7 %collective-permute-start.21 = (bf16[2,128,128]{2,1,0:T(8,128)(2,1)S(1)}, bf16[2,128,128]{2,1,0:T(8,128)(2,1)S(1)}, u32[]{:S(2)}, u32[]{:S(2)}) collective-permute-start(bf16[2,128,128]{2,1,0:T(8,128)(2,1)S(1)} %get-tuple-element.22), channel_id=1, source_target_pairs={{0,8},{8,16},{16,24},{24,32},{32,40},{40,48},{48,56},{56,0},{64,72... | collective-permute-start | bytes 196616 | tf_op jit(solution)/shard_map/ppermute | solution.py:28
  126.4 4.5 %collective-permute-start.20 = (bf16[2,128,128]{2,1,0:T(8,128)(2,1)S(1)}, bf16[2,128,128]{2,1,0:T(8,128)(2,1)S(1)}, u32[]{:S(2)}, u32[]{:S(2)}) collective-permute-start(bf16[2,128,128]{2,1,0:T(8,128)(2,1)S(1)} %get-tuple-element.22), channel_id=1, source_target_pairs={{0,56},{8,0},{16,8},{24,16},{32,24},{40,32},{48,40},{56,48},{64,12... | collective-permute-start | bytes 196616 | tf_op jit(solution)/shard_map/ppermute | solution.py:28
  130.9 14.3 %collective-permute-start.25 = (bf16[8,128,128]{2,1,0:T(8,128)(2,1)S(1)}, bf16[8,128,128]{2,1,0:T(8,128)(2,1)S(1)}, u32[]{:S(2)}, u32[]{:S(2)}) collective-permute-start(bf16[8,128,128]{2,1,0:T(8,128)(2,1)S(1)} %pad_maximum_fusion.1.e0), channel_id=1, source_target_pairs={{0,64},{8,72},{16,80},{24,88},{32,96},{40,104},{48,112},{56,120},{... | collective-permute-start | bytes 786440 | tf_op jit(solution)/shard_map/ppermute | solution.py:28
  131.7 13.5 %collective-permute-start.24 = (bf16[8,128,128]{2,1,0:T(8,128)(2,1)S(1)}, bf16[8,128,128]{2,1,0:T(8,128)(2,1)S(1)}, u32[]{:S(2)}, u32[]{:S(2)}) collective-permute-start(bf16[8,128,128]{2,1,0:T(8,128)(2,1)S(1)} %pad_maximum_fusion.1.e0), channel_id=1, source_target_pairs={{0,128},{8,136},{16,144},{24,152},{32,160},{40,168},{48,176},{56,1... | collective-permute-start | bytes 786440 | tf_op jit(solution)/shard_map/ppermute | solution.py:28
  134.8 10.5 %collective-permute-start.23 = (bf16[8,128,128]{2,1,0:T(8,128)(2,1)S(1)}, bf16[8,128,128]{2,1,0:T(8,128)(2,1)S(1)}, u32[]{:S(2)}, u32[]{:S(2)}) collective-permute-start(bf16[8,128,128]{2,1,0:T(8,128)(2,1)S(1)} %pad_maximum_fusion.1.e0), channel_id=1, source_target_pairs={{0,192},{8,200},{16,208},{24,216},{32,224},{40,232},{48,240},{56,2... | collective-permute-start | bytes 786440 | tf_op jit(solution)/shard_map/ppermute | solution.py:28
  134.8 1.2 collective-permute-start.26
  136.0 3.6 %collective-permute-start.27 = (f32[128]{0:T(128)S(1)}, f32[128]{0:T(128)S(1)}, u32[]{:S(2)}, u32[]{:S(2)}) collective-permute-start(f32[128]{0:T(128)S(1)} %add.169), channel_id=1, source_target_pairs={{0,2},{1,3},{2,0},{3,1},{4,6},{5,7},{6,4},{7,5},{8,10},{9,11},{10,... | collective-permute-start | bytes 1544 | tf_op jit(solution)/shard_map/ppermute | solution.py:314
  139.6 5.1 %collective-permute-start.28 = (f32[128]{0:T(128)S(1)}, f32[128]{0:T(128)S(1)}, u32[]{:S(2)}, u32[]{:S(2)}) collective-permute-start(f32[128]{0:T(128)S(1)} %add.170), channel_id=1, source_target_pairs={{0,4},{1,5},{2,6},{3,7},{4,0},{5,1},{6,2},{7,3},{8,12},{9,13},{10,... | collective-permute-start | bytes 1544 | tf_op jit(solution)/shard_map/ppermute | solution.py:314

commit v2 on v1

--- a/solution.py
+++ b/solution.py
@@ -12,7 +12,7 @@
 TARGETS = 1024
 NY = 4
 NZ = 8
-UNROLL = 4
+UNROLL = 8
 CHUNK = 8
 FAR = 2
 MIB = 1024 * 1024
@@ -84,8 +84,8 @@
     return jnp.concatenate(signs, axis=0), cols
 
 
-def each_pair(bounds_ref, group, body):
-    low, high = bounds_ref[group], bounds_ref[group + 1]
+def each_pair(bounds_ref, first, last, body):
+    low, high = bounds_ref[first], bounds_ref[last]
 
     def step(k, carry):
         body([low + k * UNROLL + u for u in range(UNROLL)], high)
@@ -112,59 +112,57 @@
             products = []
             for q in qs:
                 signs, cols = load_pair(codes_ref, bits_ref, masks, q, high)
-                left = jnp.concatenate([cur_b[cols[0]], cur_b[cols[1]]], axis=1)
-                products.append(jnp.dot(left, signs, preferred_element_type=jnp.float32))
+                products.append(
+                    jnp.dot(cur_b[cols[0]], signs[:B], preferred_element_type=jnp.float32)
+                    + jnp.dot(cur_b[cols[1]], signs[B:], preferred_element_type=jnp.float32)
+                )
             for q, product in zip(qs, products):
                 row = owner_ref[q] & (NZ - 1)
                 total[row] = total[row] + product
 
-        each_pair(bounds_ref, group, body)
+        each_pair(bounds_ref, group, group + 1, body)
         out[...] = total[...].astype(jnp.bfloat16)
 
 
-def backward(codes_ref, owner_ref, bounds_ref, bits_ref, errs, grad):
+def backward(codes_ref, owner_ref, bounds_ref, bits_ref, errs, table, grad):
     masks = bit_masks()
     grad[...] = jnp.zeros_like(grad)
     for group in range(NY):
-
-        def body(qs, high):
-            products, places = [], []
-            for q in qs:
-                signs, cols = load_pair(codes_ref, bits_ref, masks, q, high)
-                row = errs[group][owner_ref[q] & (NZ - 1)]
-                products.append(
-                    lax.dot_general(
-                        row, signs, (((1,), (1,)), ((), ())), preferred_element_type=jnp.float32
-                    )
-                )
-                places.append(cols)
-            for product, cols in zip(products, places):
-                for h in range(2):
-                    grad[cols[h]] = grad[cols[h]] + product[:, h * B : (h + 1) * B]
-
-        each_pair(bounds_ref, group, body)
-
-
-def shrunk(cur, grad, eta, thresh):
-    moved = cur - eta * (grad * (1.0 / 128.0))
-    return jnp.maximum(moved - thresh, 0.0) + jnp.minimum(moved + thresh, 0.0)
+        table[group * NZ : (group + 1) * NZ] = errs[group][...]
+
+    def body(qs, high):
+        products, places = [], []
+        for q in qs:
+            signs, cols = load_pair(codes_ref, bits_ref, masks, q, high)
+            row = table[owner_ref[q]]
+            products.append(jnp.dot(signs, row, preferred_element_type=jnp.float32))
+            places.append(cols)
+        for product, cols in zip(products, places):
+            for h in range(2):
+                grad[cols[h]] = grad[cols[h]] + product[h * B : (h + 1) * B]
+
+    each_pair(bounds_ref, 0, NY, body)
+
+
+def shrunk(cur, grad, scale, thresh):
+    moved = cur - scale * grad
+    return moved - jnp.maximum(jnp.minimum(moved, thresh), -thresh)
 
 
 def chunk(ref, k):
     return ref.at[pl.ds(k * CHUNK, CHUNK)]
 
 
-def first_kernel(codes, owner, bounds, bits, margins, w, far, cur_b, goal, buf, sems):
+def first_kernel(codes, owner, bounds, bits, w, far, cur_b, buf, sems):
     nchunks = w.shape[0] // CHUNK
     for k in range(nchunks):
         pltpu.make_async_copy(chunk(w, k), chunk(buf, k), sems.at[k]).start()
-    goal[...] = margins[...].T * 128.0
 
     def turn(k, carry):
         pltpu.make_async_copy(chunk(w, k), chunk(buf, k), sems.at[k]).wait()
         for u in range(CHUNK):
             j = k * CHUNK + u
-            cur_b[j] = buf[j].T.astype(jnp.bfloat16)
+            cur_b[j] = buf[j].astype(jnp.bfloat16).T
         return carry
 
     lax.fori_loop(0, nchunks, turn, 0)
@@ -172,22 +170,22 @@
 
 
 def middle_kernel(
-    codes, owner, bounds, step, pen, bits, e0, e1, e2, e3, w, far, cur_b, new, buf, grad, sem, sems
+    codes, owner, bounds, step, pen, bits, e0, e1, e2, e3, w, far, cur_b, new, buf, grad, table, sem, sems
 ):
     nchunks = w.shape[0] // CHUNK
     load = pltpu.make_async_copy(w, buf, sem)
     load.start()
-    backward(codes, owner, bounds, bits, (e0, e1, e2, e3), grad)
+    backward(codes, owner, bounds, bits, (e0, e1, e2, e3), table, grad)
     load.wait()
-    eta = step[0]
-    thresh = eta * pen[0]
+    scale = step[0] * (1.0 / 128.0)
+    thresh = step[0] * pen[0]
 
     def update(k, carry):
         for u in range(CHUNK):
             j = k * CHUNK + u
-            block = shrunk(buf[j].T, grad[j], eta, thresh)
+            block = shrunk(buf[j], grad[j], scale, thresh)
             grad[j] = block
-            cur_b[j] = block.astype(jnp.bfloat16)
+            cur_b[j] = block.astype(jnp.bfloat16).T
         pltpu.make_async_copy(chunk(grad, k), chunk(new, k), sems.at[k]).start()
         return carry
 
@@ -197,6 +195,13 @@
         pltpu.make_async_copy(chunk(grad, k), chunk(new, k), sems.at[k]).wait()
 
 
+def err_kernel(mine, other, err, squares):
+    both = (mine[...] + other[...].astype(jnp.float32)) * (1.0 / 128.0)
+    squares[...] = jnp.sum(both[0] * both[0], axis=0, keepdims=True)
+    for k in range(2):
+        err[k] = both[k].T.astype(jnp.bfloat16)
+
+
 def near_kernel(codes, owner, bounds, bits, cur_b, p1, p3):
     forward(codes, owner, bounds, bits, cur_b, (1, 3), (p1, p3))
 
@@ -205,21 +210,26 @@
     forward(codes, owner, bounds, bits, cur_b, (0,), (p0,))
 
 
+def own_goal_kernel(codes, owner, bounds, bits, cur_b, margins, p0, goal):
+    goal[...] = margins[...].T * 128.0
+    forward(codes, owner, bounds, bits, cur_b, (0,), (p0,))
+
+
 def last_kernel(
-    codes, owner, bounds, step, pen, bits, e0, e1, e2, e3, cur, out, buf, grad, sem, sems
+    codes, owner, bounds, step, pen, bits, e0, e1, e2, e3, cur, out, buf, grad, table, sem, sems
 ):
     nchunks = cur.shape[0] // CHUNK
     load = pltpu.make_async_copy(cur, buf, sem)
     load.start()
-    backward(codes, owner, bounds, bits, (e0, e1, e2, e3), grad)
+    backward(codes, owner, bounds, bits, (e0, e1, e2, e3), table, grad)
     load.wait()
-    eta = step[0]
-    thresh = eta * pen[0]
+    scale = step[0] * (1.0 / 128.0)
+    thresh = step[0] * pen[0]
 
     def update(k, carry):
         for u in range(CHUNK):
             j = k * CHUNK + u
-            grad[j] = shrunk(buf[j], grad[j], eta, thresh).T
+            grad[j] = shrunk(buf[j], grad[j], scale, thresh)
         pltpu.make_async_copy(chunk(grad, k), chunk(out, k), sems.at[k]).start()
         return carry
 
@@ -228,7 +238,7 @@
         pltpu.make_async_copy(chunk(grad, k), chunk(out, k), sems.at[k]).wait()
 
 
-def run_kernel(kernel, smem, vmem, hbm, outs, out_hbm, scratch, pairs):
+def run_kernel(kernel, smem, vmem, hbm, outs, out_hbm, scratch, pairs, grant=32):
     in_specs = [pl.BlockSpec(memory_space=pltpu.SMEM)] * len(smem)
     in_specs += [pl.BlockSpec(memory_space=pltpu.VMEM)] * len(vmem)
     in_specs += [pl.BlockSpec(memory_space=pltpu.HBM)] * len(hbm)
@@ -240,22 +250,25 @@
         in_specs=in_specs,
         out_specs=out_specs,
         scratch_shapes=scratch,
-        compiler_params=pltpu.CompilerParams(vmem_limit_bytes=(49 if hbm else 32) * MIB),
+        compiler_params=pltpu.CompilerParams(vmem_limit_bytes=grant * MIB),
         cost_estimate=pl.CostEstimate(
             flops=pairs * 16 * B * B * B, bytes_accessed=4 * 1024 * 1024, transcendentals=0
         ),
     )(*smem, *vmem, *hbm)
 
 
-def send_parts(lists, bits, cur_b, far):
+def send_parts(lists, bits, cur_b, far, margins=None):
     part = ((NZ, B, B), jnp.bfloat16)
     total = shift(far, 2, 0)
     one, three = run_kernel(near_kernel, lists, (bits, cur_b), (), [part] * 2, [], [], 80)
     up = shift(one, 1, 0)
     down = shift(three, 3, 0)
-    (own,) = run_kernel(own_kernel, lists, (bits, cur_b), (), [part], [], [], 40)
+    kernel, more, outs = own_kernel, (), [part]
+    if margins is not None:
+        kernel, more, outs = own_goal_kernel, (margins,), [part, ((B, B), jnp.float32)]
+    own, *goal = run_kernel(kernel, lists, (bits, cur_b, *more), (), outs, [], [], 40)
     total = own.astype(jnp.float32) + total.astype(jnp.float32)
-    return total + up.astype(jnp.float32) + down.astype(jnp.float32)
+    return total + up.astype(jnp.float32) + down.astype(jnp.float32), *goal
 
 
 def reduce_runs(total, goal):
@@ -265,7 +278,11 @@
         mine = mine + shift(low[at : at + 2], 0, dz).astype(jnp.float32)
     mine = jnp.stack([mine[0] - goal, mine[1]])
     other = shift(jnp.flip(mine, 0).astype(jnp.bfloat16), 0, 4)
-    return (mine + other.astype(jnp.float32)) * (1.0 / 128.0)
+    pair = ((2, B, B), jnp.bfloat16)
+    err, squares = run_kernel(
+        err_kernel, (), (mine, other), (), [pair, ((1, B), jnp.float32)], [], [], 1
+    )
+    return err, squares
 
 
 def gather_runs(two):
@@ -282,21 +299,16 @@
     table = ((nblocks, B, B), jnp.float32)
     table_b = ((nblocks, B, B), jnp.bfloat16)
     buffer = pltpu.VMEM(*table)
+    err_table = pltpu.VMEM((NY * NZ, B, B), jnp.bfloat16)
     single = pltpu.SemaphoreType.DMA
     many = pltpu.SemaphoreType.DMA((nblocks // CHUNK,))
 
-    far, cur_b, goal = run_kernel(
-        first_kernel,
-        lists,
-        (bits, margins),
-        (weights,),
-        [part, table_b, ((B, B), jnp.float32)],
-        [],
-        [buffer, many],
-        80,
-    )
-    err = reduce_runs(send_parts(lists, bits, cur_b, far), goal)
-    errs = gather_runs(err.astype(jnp.bfloat16))
+    far, cur_b = run_kernel(
+        first_kernel, lists, (bits,), (weights,), [part, table_b], [], [buffer, many], 80, 49
+    )
+    total, goal = send_parts(lists, bits, cur_b, far, margins)
+    err, _ = reduce_runs(total, goal)
+    errs = gather_runs(err)
     far, cur_b, cur = run_kernel(
         middle_kernel,
         (*lists, step_size, penalty),
@@ -304,12 +316,14 @@
         (weights,),
         [part, table_b],
         [table],
-        [buffer, buffer, single, many],
+        [buffer, buffer, err_table, single, many],
         240,
-    )
-    err = reduce_runs(send_parts(lists, bits, cur_b, far), goal)
-    errs = gather_runs(err.astype(jnp.bfloat16))
-    squares = jnp.sum(err[0] * err[0], axis=0)
+        49,
+    )
+    (total,) = send_parts(lists, bits, cur_b, far)
+    err, squares = reduce_runs(total, goal)
+    errs = gather_runs(err)
+    squares = squares.reshape(B)
     for hop in (1, 2, 4):
         squares = squares + lax.ppermute(squares, "tgt", [(k, k ^ hop) for k in range(8)])
     (out,) = run_kernel(
@@ -319,8 +333,9 @@
         (cur,),
         [],
         [table],
-        [buffer, buffer, single, many],
+        [buffer, buffer, err_table, single, many],
         200,
+        49,
     )
     return out.reshape(weights_init.shape), squares / TARGETS
 

time: 158 us -> 140 us (0.89)
  Pallas kernels: 44 us -> 32.3 us
  waiting for transfers between devices: 51.9 us -> 42.3 us
  starting transfers between devices: 50.9 us -> 55.9 us
    pallas_call x7 -> x9, Pallas kernels: 44 us -> 32.3 us  [run_kernel(): pl.pallas_call(kernel, out_shape=[jax.ShapeDtypeStruct(s, d) for s, d in...]
    ppermute x26, waiting for transfers between devices: 44.8 us -> 36.1 us  [shift(): return lax.ppermute(x, 'clus', pairs)]
    ppermute x26, starting transfers between devices: 48.1 us -> 53.3 us  [shift(): return lax.ppermute(x, 'clus', pairs)]
  transfers between devices with their start and end apart: 29 -> 29, of which waited for: 23 -> 18; matrix products, arithmetic and copies ran while one was open for 0% -> 0% of each run, Pallas kernels for 4% -> 5%
where the time goes in v2:
time: 140 us; the launch traced here: 139 us
  starting transfers between devices  55.9 us (40%)
  waiting for transfers between devices  42.3 us (30%)
  Pallas kernels  32.3 us (23%)
  other arithmetic  4.48 us (3%)
  between operations  3.03 us (2%)
  local copies, waits for them, and re-layouts  1.53 us (1%)
    ppermute x26, starting transfers between devices, shift(): return lax.ppermute(x, 'clus', pairs)  53.3 us
    ppermute x26, waiting for transfers between devices, shift(): return lax.ppermute(x, 'clus', pairs)  36.1 us
    pallas_call x9, Pallas kernels, run_kernel(): pl.pallas_call(kernel, out_shape=[jax.ShapeDtypeStruct(s, d) for s, d in...  32.3 us
    ppermute x3, waiting for transfers between devices, per_device(): lax.ppermute(squares, 'tgt', [(k, k ^ hop) for k in range(8)])  6.14 us
  transfers between devices with their start and end apart: 29, of which 18 were waited for; matrix products, arithmetic and copies ran while one was open for 0% of the time, Pallas kernels for 5%

profile of v2, /device:TPU:2, one launch (start us, length us, event | category | flops | bytes accessed | tf_op | source)
XLA Modules:
  0.0 139.4 jit_solution(4932195101743265134)
XLA Ops:
  1.3 0.7 fusion.13
  2.0 0.1 convert_reduce_fusion.1
  2.1 0.6 fusion.19
  2.8 0.1 select_reduce_fusion.2
  2.9 0.1 slice.39
  3.1 0.2 convert_reduce_fusion
  3.4 0.7 pad_add_fusion.bounds
  4.1 0.7 add_add_fusion
  4.8 0.2 select_reduce_fusion.codes
  5.0 1.3 copy-done
  6.2 4.3 %shard_map.95 = (bf16[8,128,128]{2,1,0:T(8,128)(2,1)S(1)}, bf16[64,128,128]{2,1,0:T(8,128)(2,1)S(1)}) custom-call(s32[336]{0:T(512)S(1)} %select_reduce_fusion.codes, s32[168]{0:T(256)S(1)} %broadcast_minimum_fusion.owner, s32[5]{0:T(128)S(1)} %pad_add_fusion.bounds, s32[288,8,128]{2,1,0:T(8,128)S(1)} %bitcast.25, f32[64,128,128]{2,1,0:T(8,128)} %bitcast.33), custom_call_target="tpu_custom_call" | custom-call | flops 2684354560 | bytes 4194304 | tf_op jit(solution)/shard_map/pallas_call | solution.py:247
  10.6 2.9 %collective-permute-start = (bf16[8,128,128]{2,1,0:T(8,128)(2,1)S(1)}, bf16[8,128,128]{2,1,0:T(8,128)(2,1)S(1)}, u32[]{:S(2)}, u32[]{:S(2)}) collective-permute-start(bf16[8,128,128]{2,1,0:T(8,128)(2,1)S(1)} %get-tuple-element.18), channel_id=1, source_target_pairs={{0,128},{8,136},{16,144},{24,152},{32,160},{40,168},{48,176},{56,1... | collective-permute-start | bytes 786440 | tf_op jit(solution)/shard_map/ppermute | solution.py:28
  13.5 3.4 %shard_map.97 = (bf16[8,128,128]{2,1,0:T(8,128)(2,1)S(1)}, bf16[8,128,128]{2,1,0:T(8,128)(2,1)S(1)}) custom-call(s32[336]{0:T(512)S(1)} %select_reduce_fusion.codes, s32[168]{0:T(256)S(1)} %broadcast_minimum_fusion.owner, s32[5]{0:T(128)S(1)} %pad_add_fusion.bounds, s32[288,8,128]{2,1,0:T(8,128)S(1)} %bitcast.26, ...), custom_call_target="tpu_custom_call" | custom-call | flops 2684354560 | bytes 4194304 | tf_op jit(solution)/shard_map/pallas_call | solution.py:247
  17.0 0.7 collective-permute-start.1
  17.7 2.6 %collective-permute-start.2 = (bf16[8,128,128]{2,1,0:T(8,128)(2,1)S(1)}, bf16[8,128,128]{2,1,0:T(8,128)(2,1)S(1)}, u32[]{:S(2)}, u32[]{:S(2)}) collective-permute-start(bf16[8,128,128]{2,1,0:T(8,128)(2,1)S(1)} %get-tuple-element.20), channel_id=1, source_target_pairs={{0,192},{8,200},{16,208},{24,216},{32,224},{40,232},{48,240},{56,2... | collective-permute-start | bytes 786440 | tf_op jit(solution)/shard_map/ppermute | solution.py:28
  20.3 2.1 %shard_map.96 = (bf16[8,128,128]{2,1,0:T(8,128)(2,1)S(1)}, f32[128,128]{1,0:T(8,128)S(1)}) custom-call(s32[336]{0:T(512)S(1)} %select_reduce_fusion.codes, s32[168]{0:T(256)S(1)} %broadcast_minimum_fusion.owner, s32[5]{0:T(128)S(1)} %pad_add_fusion.bounds, s32[288,8,128]{2,1,0:T(8,128)S(1)} %bitcast.27, bf16[64,128,128]{2,1,0:T(8,128)(2,1)S(1)} %get-tuple-element.16.cur_b, ...), custom_call_target="tpu_custom_call" | custom-call | flops 1342177280 | bytes 4194304 | tf_op jit(solution)/shard_map/pallas_call | solution.py:247
  22.4 3.6 %collective-permute-done.1 = bf16[8,128,128]{2,1,0:T(8,128)(2,1)S(1)} collective-permute-done((bf16[8,128,128]{2,1,0:T(8,128)(2,1)S(1)}, bf16[8,128,128]{2,1,0:T(8,128)(2,1)S(1)}, u32[]{:S(2)}, u32[]{:S(2)}) %collective-permute-start.1) | collective-permute-done | bytes 262176 | tf_op jit(solution)/shard_map/ppermute | solution.py:28
  26.0 0.2 collective-permute-done.2
  26.2 0.1 fusion.18
  26.4 3.2 %collective-permute-start.3 = (bf16[2,128,128]{2,1,0:T(8,128)(2,1)S(1)}, bf16[2,128,128]{2,1,0:T(8,128)(2,1)S(1)}, u32[]{:S(2)}, u32[]{:S(2)}) collective-permute-start(bf16[2,128,128]{2,1,0:T(8,128)(2,1)S(1)} %get-tuple-element.39), channel_id=1, source_target_pairs={{0,16},{8,24},{16,32},{24,40},{32,48},{40,56},{48,0},{56,8},{64,80... | collective-permute-start | bytes 196616 | tf_op jit(solution)/shard_map/ppermute | solution.py:28
  29.6 2.9 %collective-permute-start.5 = (bf16[2,128,128]{2,1,0:T(8,128)(2,1)S(1)}, bf16[2,128,128]{2,1,0:T(8,128)(2,1)S(1)}, u32[]{:S(2)}, u32[]{:S(2)}) collective-permute-start(bf16[2,128,128]{2,1,0:T(8,128)(2,1)S(1)} %get-tuple-element.40), channel_id=1, source_target_pairs={{0,56},{8,0},{16,8},{24,16},{32,24},{40,32},{48,40},{56,48},{64,12... | collective-permute-start | bytes 196616 | tf_op jit(solution)/shard_map/ppermute | solution.py:28
  32.5 4.8 %collective-permute-done.3 = bf16[2,128,128]{2,1,0:T(8,128)(2,1)S(1)} collective-permute-done((bf16[2,128,128]{2,1,0:T(8,128)(2,1)S(1)}, bf16[2,128,128]{2,1,0:T(8,128)(2,1)S(1)}, u32[]{:S(2)}, u32[]{:S(2)}) %collective-permute-start.3) | collective-permute-done | bytes 65568 | tf_op jit(solution)/shard_map/ppermute | solution.py:28
  37.3 0.7 collective-permute-done.4
  38.1 5.7 %collective-permute-start.6 = (bf16[2,128,128]{2,1,0:T(8,128)(2,1)S(1)}, bf16[2,128,128]{2,1,0:T(8,128)(2,1)S(1)}, u32[]{:S(2)}, u32[]{:S(2)}) collective-permute-start(bf16[2,128,128]{2,1,0:T(8,128)(2,1)S(1)} %rev.12), channel_id=1, source_target_pairs={{0,32},{8,40},{16,48},{24,56},{32,0},{40,8},{48,16},{56,24},{64,96... | collective-permute-start | bytes 196616 | tf_op jit(solution)/shard_map/ppermute | solution.py:28
  43.9 2.8 %collective-permute-done.6.other = bf16[2,128,128]{2,1,0:T(8,128)(2,1)S(1)} collective-permute-done((bf16[2,128,128]{2,1,0:T(8,128)(2,1)S(1)}, bf16[2,128,128]{2,1,0:T(8,128)(2,1)S(1)}, u32[]{:S(2)}, u32[]{:S(2)}) %collective-permute-start.6) | collective-permute-done | bytes 65568 | tf_op jit(solution)/shard_map/ppermute | solution.py:28
  46.7 0.5 shard_map.98
  47.2 2.9 %collective-permute-start.9 = (bf16[2,128,128]{2,1,0:T(8,128)(2,1)S(1)}, bf16[2,128,128]{2,1,0:T(8,128)(2,1)S(1)}, u32[]{:S(2)}, u32[]{:S(2)}) collective-permute-start(bf16[2,128,128]{2,1,0:T(8,128)(2,1)S(1)} %get-tuple-element.22), channel_id=1, source_target_pairs={{0,48},{8,56},{16,0},{24,8},{32,16},{40,24},{48,32},{56,40},{64,11... | collective-permute-start | bytes 196616 | tf_op jit(solution)/shard_map/ppermute | solution.py:28
  50.1 3.2 %collective-permute-start.7 = (bf16[2,128,128]{2,1,0:T(8,128)(2,1)S(1)}, bf16[2,128,128]{2,1,0:T(8,128)(2,1)S(1)}, u32[]{:S(2)}, u32[]{:S(2)}) collective-permute-start(bf16[2,128,128]{2,1,0:T(8,128)(2,1)S(1)} %get-tuple-element.22), channel_id=1, source_target_pairs={{0,56},{8,0},{16,8},{24,16},{32,24},{40,32},{48,40},{56,48},{64,12... | collective-permute-start | bytes 196616 | tf_op jit(solution)/shard_map/ppermute | solution.py:28
  53.3 1.9 %collective-permute-done.7 = bf16[2,128,128]{2,1,0:T(8,128)(2,1)S(1)} collective-permute-done((bf16[2,128,128]{2,1,0:T(8,128)(2,1)S(1)}, bf16[2,128,128]{2,1,0:T(8,128)(2,1)S(1)}, u32[]{:S(2)}, u32[]{:S(2)}) %collective-permute-start.7) | collective-permute-done | bytes 65568 | tf_op jit(solution)/shard_map/ppermute | solution.py:28
  55.3 0.3 collective-permute-done.8
  55.6 1.0 collective-permute-start.12
  56.6 3.5 %collective-permute-start.11 = (bf16[8,128,128]{2,1,0:T(8,128)(2,1)S(1)}, bf16[8,128,128]{2,1,0:T(8,128)(2,1)S(1)}, u32[]{:S(2)}, u32[]{:S(2)}) collective-permute-start(bf16[8,128,128]{2,1,0:T(8,128)(2,1)S(1)} %constant_dynamic-update-slice_fusion.e0), channel_id=1, source_target_pairs={{0,128},{8,136},{16,144},{24,152},{32,160},{40,168},{48,176},{56,1... | collective-permute-start | bytes 786440 | tf_op jit(solution)/shard_map/ppermute | solution.py:28
  60.1 0.3 collective-permute-start.10
  61.7 3.1 %collective-permute-done.12.e3 = bf16[8,128,128]{2,1,0:T(8,128)(2,1)S(1)} collective-permute-done((bf16[8,128,128]{2,1,0:T(8,128)(2,1)S(1)}, bf16[8,128,128]{2,1,0:T(8,128)(2,1)S(1)}, u32[]{:S(2)}, u32[]{:S(2)}) %collective-permute-start.12) | collective-permute-done | bytes 262176 | tf_op jit(solution)/shard_map/ppermute | solution.py:28
  64.8 2.8 %collective-permute-done.11.e2 = bf16[8,128,128]{2,1,0:T(8,128)(2,1)S(1)} collective-permute-done((bf16[8,128,128]{2,1,0:T(8,128)(2,1)S(1)}, bf16[8,128,128]{2,1,0:T(8,128)(2,1)S(1)}, u32[]{:S(2)}, u32[]{:S(2)}) %collective-permute-start.11) | collective-permute-done | bytes 262176 | tf_op jit(solution)/shard_map/ppermute | solution.py:28
  67.6 8.5 %shard_map.99 = (bf16[8,128,128]{2,1,0:T(8,128)(2,1)S(1)}, bf16[64,128,128]{2,1,0:T(8,128)(2,1)S(1)}, f32[64,128,128]{2,1,0:T(8,128)}) custom-call(s32[336]{0:T(512)S(1)} %select_reduce_fusion.codes, s32[168]{0:T(256)S(1)} %broadcast_minimum_fusion.owner, s32[5]{0:T(128)S(1)} %pad_add_fusion.bounds, f32[1]{0:T(128)S(6)} %copy.17.step, f32[1]{0:T(128)S(6)} %copy.18.pen, ...), custom_call_target="tpu_custom_call" | custom-call | flops 8053063680 | bytes 4194304 | tf_op jit(solution)/shard_map/pallas_call | solution.py:247
  76.1 3.4 %shard_map.101 = (bf16[8,128,128]{2,1,0:T(8,128)(2,1)S(1)}, bf16[8,128,128]{2,1,0:T(8,128)(2,1)S(1)}) custom-call(s32[336]{0:T(512)S(1)} %select_reduce_fusion.codes, s32[168]{0:T(256)S(1)} %broadcast_minimum_fusion.owner, s32[5]{0:T(128)S(1)} %pad_add_fusion.bounds, s32[288,8,128]{2,1,0:T(8,128)S(1)} %bitcast.29, ...), custom_call_target="tpu_custom_call" | custom-call | flops 2684354560 | bytes 4194304 | tf_op jit(solution)/shard_map/pallas_call | solution.py:247
  79.5 0.8 collective-permute-start.14
  80.3 4.0 %collective-permute-start.15 = (bf16[8,128,128]{2,1,0:T(8,128)(2,1)S(1)}, bf16[8,128,128]{2,1,0:T(8,128)(2,1)S(1)}, u32[]{:S(2)}, u32[]{:S(2)}) collective-permute-start(bf16[8,128,128]{2,1,0:T(8,128)(2,1)S(1)} %get-tuple-element.26), channel_id=1, source_target_pairs={{0,192},{8,200},{16,208},{24,216},{32,224},{40,232},{48,240},{56,2... | collective-permute-start | bytes 786440 | tf_op jit(solution)/shard_map/ppermute | solution.py:28
  84.3 1.4 collective-permute-start.13
  85.7 2.0 %shard_map.100 = bf16[8,128,128]{2,1,0:T(8,128)(2,1)S(1)} custom-call(s32[336]{0:T(512)S(1)} %select_reduce_fusion.codes, s32[168]{0:T(256)S(1)} %broadcast_minimum_fusion.owner, s32[5]{0:T(128)S(1)} %pad_add_fusion.bounds, s32[288,8,128]{2,1,0:T(8,128)S(1)} %bitcast.30, bf16[64,128,128]{2,1,0:T(8,128)(2,1)S(1)} %get-tuple-element.23.cur_b), custom_call_target="tpu_custom_call" | custom-call | flops 1342177280 | bytes 4194304 | tf_op jit(solution)/shard_map/pallas_call | solution.py:247
  87.7 2.9 %collective-permute-done.14 = bf16[8,128,128]{2,1,0:T(8,128)(2,1)S(1)} collective-permute-done((bf16[8,128,128]{2,1,0:T(8,128)(2,1)S(1)}, bf16[8,128,128]{2,1,0:T(8,128)(2,1)S(1)}, u32[]{:S(2)}, u32[]{:S(2)}) %collective-permute-start.14) | collective-permute-done | bytes 262176 | tf_op jit(solution)/shard_map/ppermute | solution.py:28
  90.6 1.1 collective-permute-done.15
  91.7 1.7 %collective-permute-done.13 = bf16[8,128,128]{2,1,0:T(8,128)(2,1)S(1)} collective-permute-done((bf16[8,128,128]{2,1,0:T(8,128)(2,1)S(1)}, bf16[8,128,128]{2,1,0:T(8,128)(2,1)S(1)}, u32[]{:S(2)}, u32[]{:S(2)}) %collective-permute-start.13) | collective-permute-done | bytes 262176 | tf_op jit(solution)/shard_map/ppermute | solution.py:28
  93.4 0.1 fusion.17
  93.7 1.5 %collective-permute-start.18 = (bf16[2,128,128]{2,1,0:T(8,128)(2,1)S(1)}, bf16[2,128,128]{2,1,0:T(8,128)(2,1)S(1)}, u32[]{:S(2)}, u32[]{:S(2)}) collective-permute-start(bf16[2,128,128]{2,1,0:T(8,128)(2,1)S(1)} %get-tuple-element.37), channel_id=1, source_target_pairs={{0,56},{8,0},{16,8},{24,16},{32,24},{40,32},{48,40},{56,48},{64,12... | collective-permute-start | bytes 196616 | tf_op jit(solution)/shard_map/ppermute | solution.py:28
  95.2 2.2 %collective-permute-start.17 = (bf16[2,128,128]{2,1,0:T(8,128)(2,1)S(1)}, bf16[2,128,128]{2,1,0:T(8,128)(2,1)S(1)}, u32[]{:S(2)}, u32[]{:S(2)}) collective-permute-start(bf16[2,128,128]{2,1,0:T(8,128)(2,1)S(1)} %get-tuple-element.38), channel_id=1, source_target_pairs={{0,8},{8,16},{16,24},{24,32},{32,40},{40,48},{48,56},{56,0},{64,72... | collective-permute-start | bytes 196616 | tf_op jit(solution)/shard_map/ppermute | solution.py:28
  97.4 3.3 %collective-permute-done.16 = bf16[2,128,128]{2,1,0:T(8,128)(2,1)S(1)} collective-permute-done((bf16[2,128,128]{2,1,0:T(8,128)(2,1)S(1)}, bf16[2,128,128]{2,1,0:T(8,128)(2,1)S(1)}, u32[]{:S(2)}, u32[]{:S(2)}) %collective-permute-start.16) | collective-permute-done | bytes 65568 | tf_op jit(solution)/shard_map/ppermute | solution.py:28
  100.7 0.2 collective-permute-done.17
  101.0 4.7 %collective-permute-start.19 = (bf16[2,128,128]{2,1,0:T(8,128)(2,1)S(1)}, bf16[2,128,128]{2,1,0:T(8,128)(2,1)S(1)}, u32[]{:S(2)}, u32[]{:S(2)}) collective-permute-start(bf16[2,128,128]{2,1,0:T(8,128)(2,1)S(1)} %rev.11), channel_id=1, source_target_pairs={{0,32},{8,40},{16,48},{24,56},{32,0},{40,8},{48,16},{56,24},{64,96... | collective-permute-start | bytes 196616 | tf_op jit(solution)/shard_map/ppermute | solution.py:28
  105.7 3.7 %collective-permute-done.19.other = bf16[2,128,128]{2,1,0:T(8,128)(2,1)S(1)} collective-permute-done((bf16[2,128,128]{2,1,0:T(8,128)(2,1)S(1)}, bf16[2,128,128]{2,1,0:T(8,128)(2,1)S(1)}, u32[]{:S(2)}, u32[]{:S(2)}) %collective-permute-start.19) | collective-permute-done | bytes 65568 | tf_op jit(solution)/shard_map/ppermute | solution.py:28
  109.5 0.1 shard_map.102
  109.6 1.9 %collective-permute-start.22 = (bf16[2,128,128]{2,1,0:T(8,128)(2,1)S(1)}, bf16[2,128,128]{2,1,0:T(8,128)(2,1)S(1)}, u32[]{:S(2)}, u32[]{:S(2)}) collective-permute-start(bf16[2,128,128]{2,1,0:T(8,128)(2,1)S(1)} %get-tuple-element.27), channel_id=1, source_target_pairs={{0,48},{8,56},{16,0},{24,8},{32,16},{40,24},{48,32},{56,40},{64,11... | collective-permute-start | bytes 196616 | tf_op jit(solution)/shard_map/ppermute | solution.py:28
  111.5 2.0 %collective-permute-start.21 = (bf16[2,128,128]{2,1,0:T(8,128)(2,1)S(1)}, bf16[2,128,128]{2,1,0:T(8,128)(2,1)S(1)}, u32[]{:S(2)}, u32[]{:S(2)}) collective-permute-start(bf16[2,128,128]{2,1,0:T(8,128)(2,1)S(1)} %get-tuple-element.27), channel_id=1, source_target_pairs={{0,8},{8,16},{16,24},{24,32},{32,40},{40,48},{48,56},{56,0},{64,72... | collective-permute-start | bytes 196616 | tf_op jit(solution)/shard_map/ppermute | solution.py:28
  113.5 1.2 collective-permute-start.20
  114.7 3.0 %collective-permute-done.20 = bf16[2,128,128]{2,1,0:T(8,128)(2,1)S(1)} collective-permute-done((bf16[2,128,128]{2,1,0:T(8,128)(2,1)S(1)}, bf16[2,128,128]{2,1,0:T(8,128)(2,1)S(1)}, u32[]{:S(2)}, u32[]{:S(2)}) %collective-permute-start.20) | collective-permute-done | bytes 65568 | tf_op jit(solution)/shard_map/ppermute | solution.py:28
  117.8 1.1 collective-permute-start.25
  118.9 3.3 %collective-permute-start.24 = (bf16[8,128,128]{2,1,0:T(8,128)(2,1)S(1)}, bf16[8,128,128]{2,1,0:T(8,128)(2,1)S(1)}, u32[]{:S(2)}, u32[]{:S(2)}) collective-permute-start(bf16[8,128,128]{2,1,0:T(8,128)(2,1)S(1)} %constant_dynamic-update-slice_fusion.4.e0), channel_id=1, source_target_pairs={{0,128},{8,136},{16,144},{24,152},{32,160},{40,168},{48,176},{56,1... | collective-permute-start | bytes 786440 | tf_op jit(solution)/shard_map/ppermute | solution.py:28
  122.2 0.5 collective-permute-start.27
  122.8 3.1 %collective-permute-done.27 = f32[128]{0:T(128)S(1)} collective-permute-done((f32[128]{0:T(128)S(1)}, f32[128]{0:T(128)S(1)}, u32[]{:S(2)}, u32[]{:S(2)}) %collective-permute-start.27) | collective-permute-done | bytes 544 | tf_op jit(solution)/shard_map/ppermute | solution.py:328
  125.9 2.0 %collective-permute-start.28 = (f32[128]{0:T(128)S(1)}, f32[128]{0:T(128)S(1)}, u32[]{:S(2)}, u32[]{:S(2)}) collective-permute-start(f32[128]{0:T(128)S(1)} %add.162), channel_id=1, source_target_pairs={{0,4},{1,5},{2,6},{3,7},{4,0},{5,1},{6,2},{7,3},{8,12},{9,13},{10,... | collective-permute-start | bytes 1544 | tf_op jit(solution)/shard_map/ppermute | solution.py:328
  127.9 3.0 %collective-permute-done.28 = f32[128]{0:T(128)S(1)} collective-permute-done((f32[128]{0:T(128)S(1)}, f32[128]{0:T(128)S(1)}, u32[]{:S(2)}, u32[]{:S(2)}) %collective-permute-start.28) | collective-permute-done | bytes 544 | tf_op jit(solution)/shard_map/ppermute | solution.py:328
  130.9 0.5 add_multiply_fusion
  131.5 7.8 %shard_map.103 = f32[64,128,128]{2,1,0:T(8,128)} custom-call(s32[336]{0:T(512)S(1)} %select_reduce_fusion.codes, s32[168]{0:T(256)S(1)} %broadcast_minimum_fusion.owner, s32[5]{0:T(128)S(1)} %pad_add_fusion.bounds, f32[1]{0:T(128)S(6)} %copy.17.step, f32[1]{0:T(128)S(6)} %copy.18.pen, s32[288,8,128]{2,1,0:T(8,128)S(1)} %bitcast.31, ...), custom_call_target="tpu_custom_call" | custom-call | flops 6710886400 | bytes 4194304 | tf_op jit(solution)/shard_map/pallas_call | solution.py:247
  (47 shorter events, 0.6 us)
Async XLA Ops:
  5.0 1.3 copy-start
  10.6 11.8 %collective-permute-start = (bf16[8,128,128]{2,1,0:T(8,128)(2,1)S(1)}, bf16[8,128,128]{2,1,0:T(8,128)(2,1)S(1)}, u32[]{:S(2)}, u32[]{:S(2)}) collective-permute-start(bf16[8,128,128]{2,1,0:T(8,128)(2,1)S(1)} %get-tuple-element.18), channel_id=1, source_target_pairs={{0,128},{8,136},{16,144},{24,152},{32,160},{40,168},{48,176},{56,1... | collective-permute-start | bytes 786440 | tf_op jit(solution)/shard_map/ppermute | solution.py:28
  13.5 6.8 %copy-start.2 = (f32[128,128]{1,0:T(8,128)S(1)}, f32[128,128]{1,0:T(8,128)}, u32[]{:S(2)}) copy-start(f32[128,128]{1,0:T(8,128)} %margins.1) | copy-start | bytes 196612
  17.0 9.1 %collective-permute-start.1 = (bf16[8,128,128]{2,1,0:T(8,128)(2,1)S(1)}, bf16[8,128,128]{2,1,0:T(8,128)(2,1)S(1)}, u32[]{:S(2)}, u32[]{:S(2)}) collective-permute-start(bf16[8,128,128]{2,1,0:T(8,128)(2,1)S(1)} %get-tuple-element.19), channel_id=1, source_target_pairs={{0,64},{8,72},{16,80},{24,88},{32,96},{40,104},{48,112},{56,120},{... | collective-permute-start | bytes 786440 | tf_op jit(solution)/shard_map/ppermute | solution.py:28
  17.7 49.9 %copy-start.1 = (s32[288,128,8]{1,2,0:T(8,128)S(1)}, s32[288,128,8]{1,2,0:T(8,128)}, u32[]{:S(2)}) copy-start(s32[288,128,8]{1,2,0:T(8,128)} %param.10) | copy-start | bytes 3538948
  17.7 8.5 %collective-permute-start.2 = (bf16[8,128,128]{2,1,0:T(8,128)(2,1)S(1)}, bf16[8,128,128]{2,1,0:T(8,128)(2,1)S(1)}, u32[]{:S(2)}, u32[]{:S(2)}) collective-permute-start(bf16[8,128,128]{2,1,0:T(8,128)(2,1)S(1)} %get-tuple-element.20), channel_id=1, source_target_pairs={{0,192},{8,200},{16,208},{24,216},{32,224},{40,232},{48,240},{56,2... | collective-permute-start | bytes 786440 | tf_op jit(solution)/shard_map/ppermute | solution.py:28
  26.4 10.9 %collective-permute-start.3 = (bf16[2,128,128]{2,1,0:T(8,128)(2,1)S(1)}, bf16[2,128,128]{2,1,0:T(8,128)(2,1)S(1)}, u32[]{:S(2)}, u32[]{:S(2)}) collective-permute-start(bf16[2,128,128]{2,1,0:T(8,128)(2,1)S(1)} %get-tuple-element.39), channel_id=1, source_target_pairs={{0,16},{8,24},{16,32},{24,40},{32,48},{40,56},{48,0},{56,8},{64,80... | collective-permute-start | bytes 196616 | tf_op jit(solution)/shard_map/ppermute | solution.py:28
  29.6 7.7 %collective-permute-start.5 = (bf16[2,128,128]{2,1,0:T(8,128)(2,1)S(1)}, bf16[2,128,128]{2,1,0:T(8,128)(2,1)S(1)}, u32[]{:S(2)}, u32[]{:S(2)}) collective-permute-start(bf16[2,128,128]{2,1,0:T(8,128)(2,1)S(1)} %get-tuple-element.40), channel_id=1, source_target_pairs={{0,56},{8,0},{16,8},{24,16},{32,24},{40,32},{48,40},{56,48},{64,12... | collective-permute-start | bytes 196616 | tf_op jit(solution)/shard_map/ppermute | solution.py:28
  32.5 5.5 %collective-permute-start.4 = (bf16[2,128,128]{2,1,0:T(8,128)(2,1)S(1)}, bf16[2,128,128]{2,1,0:T(8,128)(2,1)S(1)}, u32[]{:S(2)}, u32[]{:S(2)}) collective-permute-start(bf16[2,128,128]{2,1,0:T(8,128)(2,1)S(1)} %get-tuple-element.41), channel_id=1, source_target_pairs={{0,8},{8,16},{16,24},{24,32},{32,40},{40,48},{48,56},{56,0},{64,72... | collective-permute-start | bytes 196616 | tf_op jit(solution)/shard_map/ppermute | solution.py:28
  38.1 8.6 %collective-permute-start.6 = (bf16[2,128,128]{2,1,0:T(8,128)(2,1)S(1)}, bf16[2,128,128]{2,1,0:T(8,128)(2,1)S(1)}, u32[]{:S(2)}, u32[]{:S(2)}) collective-permute-start(bf16[2,128,128]{2,1,0:T(8,128)(2,1)S(1)} %rev.12), channel_id=1, source_target_pairs={{0,32},{8,40},{16,48},{24,56},{32,0},{40,8},{48,16},{56,24},{64,96... | collective-permute-start | bytes 196616 | tf_op jit(solution)/shard_map/ppermute | solution.py:28
  47.2 8.4 %collective-permute-start.9 = (bf16[2,128,128]{2,1,0:T(8,128)(2,1)S(1)}, bf16[2,128,128]{2,1,0:T(8,128)(2,1)S(1)}, u32[]{:S(2)}, u32[]{:S(2)}) collective-permute-start(bf16[2,128,128]{2,1,0:T(8,128)(2,1)S(1)} %get-tuple-element.22), channel_id=1, source_target_pairs={{0,48},{8,56},{16,0},{24,8},{32,16},{40,24},{48,32},{56,40},{64,11... | collective-permute-start | bytes 196616 | tf_op jit(solution)/shard_map/ppermute | solution.py:28
  50.1 5.5 %collective-permute-start.8 = (bf16[2,128,128]{2,1,0:T(8,128)(2,1)S(1)}, bf16[2,128,128]{2,1,0:T(8,128)(2,1)S(1)}, u32[]{:S(2)}, u32[]{:S(2)}) collective-permute-start(bf16[2,128,128]{2,1,0:T(8,128)(2,1)S(1)} %get-tuple-element.22), channel_id=1, source_target_pairs={{0,8},{8,16},{16,24},{24,32},{32,40},{40,48},{48,56},{56,0},{64,72... | collective-permute-start | bytes 196616 | tf_op jit(solution)/shard_map/ppermute | solution.py:28
  50.1 5.1 %collective-permute-start.7 = (bf16[2,128,128]{2,1,0:T(8,128)(2,1)S(1)}, bf16[2,128,128]{2,1,0:T(8,128)(2,1)S(1)}, u32[]{:S(2)}, u32[]{:S(2)}) collective-permute-start(bf16[2,128,128]{2,1,0:T(8,128)(2,1)S(1)} %get-tuple-element.22), channel_id=1, source_target_pairs={{0,56},{8,0},{16,8},{24,16},{32,24},{40,32},{48,40},{56,48},{64,12... | collective-permute-start | bytes 196616 | tf_op jit(solution)/shard_map/ppermute | solution.py:28
  55.6 9.2 %collective-permute-start.12 = (bf16[8,128,128]{2,1,0:T(8,128)(2,1)S(1)}, bf16[8,128,128]{2,1,0:T(8,128)(2,1)S(1)}, u32[]{:S(2)}, u32[]{:S(2)}) collective-permute-start(bf16[8,128,128]{2,1,0:T(8,128)(2,1)S(1)} %constant_dynamic-update-slice_fusion.e0), channel_id=1, source_target_pairs={{0,64},{8,72},{16,80},{24,88},{32,96},{40,104},{48,112},{56,120},{... | collective-permute-start | bytes 786440 | tf_op jit(solution)/shard_map/ppermute | solution.py:28
  56.6 11.0 %collective-permute-start.11 = (bf16[8,128,128]{2,1,0:T(8,128)(2,1)S(1)}, bf16[8,128,128]{2,1,0:T(8,128)(2,1)S(1)}, u32[]{:S(2)}, u32[]{:S(2)}) collective-permute-start(bf16[8,128,128]{2,1,0:T(8,128)(2,1)S(1)} %constant_dynamic-update-slice_fusion.e0), channel_id=1, source_target_pairs={{0,128},{8,136},{16,144},{24,152},{32,160},{40,168},{48,176},{56,1... | collective-permute-start | bytes 786440 | tf_op jit(solution)/shard_map/ppermute | solution.py:28
  60.1 7.5 %collective-permute-start.10 = (bf16[8,128,128]{2,1,0:T(8,128)(2,1)S(1)}, bf16[8,128,128]{2,1,0:T(8,128)(2,1)S(1)}, u32[]{:S(2)}, u32[]{:S(2)}) collective-permute-start(bf16[8,128,128]{2,1,0:T(8,128)(2,1)S(1)} %constant_dynamic-update-slice_fusion.e0), channel_id=1, source_target_pairs={{0,192},{8,200},{16,208},{24,216},{32,224},{40,232},{48,240},{56,2... | collective-permute-start | bytes 786440 | tf_op jit(solution)/shard_map/ppermute | solution.py:28
  79.5 11.1 %collective-permute-start.14 = (bf16[8,128,128]{2,1,0:T(8,128)(2,1)S(1)}, bf16[8,128,128]{2,1,0:T(8,128)(2,1)S(1)}, u32[]{:S(2)}, u32[]{:S(2)}) collective-permute-start(bf16[8,128,128]{2,1,0:T(8,128)(2,1)S(1)} %get-tuple-element.25), channel_id=1, source_target_pairs={{0,64},{8,72},{16,80},{24,88},{32,96},{40,104},{48,112},{56,120},{... | collective-permute-start | bytes 786440 | tf_op jit(solution)/shard_map/ppermute | solution.py:28
  80.3 11.4 %collective-permute-start.15 = (bf16[8,128,128]{2,1,0:T(8,128)(2,1)S(1)}, bf16[8,128,128]{2,1,0:T(8,128)(2,1)S(1)}, u32[]{:S(2)}, u32[]{:S(2)}) collective-permute-start(bf16[8,128,128]{2,1,0:T(8,128)(2,1)S(1)} %get-tuple-element.26), channel_id=1, source_target_pairs={{0,192},{8,200},{16,208},{24,216},{32,224},{40,232},{48,240},{56,2... | collective-permute-start | bytes 786440 | tf_op jit(solution)/shard_map/ppermute | solution.py:28
  84.3 9.1 %collective-permute-start.13 = (bf16[8,128,128]{2,1,0:T(8,128)(2,1)S(1)}, bf16[8,128,128]{2,1,0:T(8,128)(2,1)S(1)}, u32[]{:S(2)}, u32[]{:S(2)}) collective-permute-start(bf16[8,128,128]{2,1,0:T(8,128)(2,1)S(1)} %get-tuple-element.24), channel_id=1, source_target_pairs={{0,128},{8,136},{16,144},{24,152},{32,160},{40,168},{48,176},{56,1... | collective-permute-start | bytes 786440 | tf_op jit(solution)/shard_map/ppermute | solution.py:28
  93.6 7.1 %collective-permute-start.16 = (bf16[2,128,128]{2,1,0:T(8,128)(2,1)S(1)}, bf16[2,128,128]{2,1,0:T(8,128)(2,1)S(1)}, u32[]{:S(2)}, u32[]{:S(2)}) collective-permute-start(bf16[2,128,128]{2,1,0:T(8,128)(2,1)S(1)} %get-tuple-element.36), channel_id=1, source_target_pairs={{0,16},{8,24},{16,32},{24,40},{32,48},{40,56},{48,0},{56,8},{64,80... | collective-permute-start | bytes 196616 | tf_op jit(solution)/shard_map/ppermute | solution.py:28
  93.7 7.0 %collective-permute-start.18 = (bf16[2,128,128]{2,1,0:T(8,128)(2,1)S(1)}, bf16[2,128,128]{2,1,0:T(8,128)(2,1)S(1)}, u32[]{:S(2)}, u32[]{:S(2)}) collective-permute-start(bf16[2,128,128]{2,1,0:T(8,128)(2,1)S(1)} %get-tuple-element.37), channel_id=1, source_target_pairs={{0,56},{8,0},{16,8},{24,16},{32,24},{40,32},{48,40},{56,48},{64,12... | collective-permute-start | bytes 196616 | tf_op jit(solution)/shard_map/ppermute | solution.py:28
  95.2 5.7 %collective-permute-start.17 = (bf16[2,128,128]{2,1,0:T(8,128)(2,1)S(1)}, bf16[2,128,128]{2,1,0:T(8,128)(2,1)S(1)}, u32[]{:S(2)}, u32[]{:S(2)}) collective-permute-start(bf16[2,128,128]{2,1,0:T(8,128)(2,1)S(1)} %get-tuple-element.38), channel_id=1, source_target_pairs={{0,8},{8,16},{16,24},{24,32},{32,40},{40,48},{48,56},{56,0},{64,72... | collective-permute-start | bytes 196616 | tf_op jit(solution)/shard_map/ppermute | solution.py:28
  101.0 8.5 %collective-permute-start.19 = (bf16[2,128,128]{2,1,0:T(8,128)(2,1)S(1)}, bf16[2,128,128]{2,1,0:T(8,128)(2,1)S(1)}, u32[]{:S(2)}, u32[]{:S(2)}) collective-permute-start(bf16[2,128,128]{2,1,0:T(8,128)(2,1)S(1)} %rev.11), channel_id=1, source_target_pairs={{0,32},{8,40},{16,48},{24,56},{32,0},{40,8},{48,16},{56,24},{64,96... | collective-permute-start | bytes 196616 | tf_op jit(solution)/shard_map/ppermute | solution.py:28
  109.6 8.2 %collective-permute-start.22 = (bf16[2,128,128]{2,1,0:T(8,128)(2,1)S(1)}, bf16[2,128,128]{2,1,0:T(8,128)(2,1)S(1)}, u32[]{:S(2)}, u32[]{:S(2)}) collective-permute-start(bf16[2,128,128]{2,1,0:T(8,128)(2,1)S(1)} %get-tuple-element.27), channel_id=1, source_target_pairs={{0,48},{8,56},{16,0},{24,8},{32,16},{40,24},{48,32},{56,40},{64,11... | collective-permute-start | bytes 196616 | tf_op jit(solution)/shard_map/ppermute | solution.py:28
  111.5 6.3 %collective-permute-start.21 = (bf16[2,128,128]{2,1,0:T(8,128)(2,1)S(1)}, bf16[2,128,128]{2,1,0:T(8,128)(2,1)S(1)}, u32[]{:S(2)}, u32[]{:S(2)}) collective-permute-start(bf16[2,128,128]{2,1,0:T(8,128)(2,1)S(1)} %get-tuple-element.27), channel_id=1, source_target_pairs={{0,8},{8,16},{16,24},{24,32},{32,40},{40,48},{48,56},{56,0},{64,72... | collective-permute-start | bytes 196616 | tf_op jit(solution)/shard_map/ppermute | solution.py:28
  113.5 4.3 %collective-permute-start.20 = (bf16[2,128,128]{2,1,0:T(8,128)(2,1)S(1)}, bf16[2,128,128]{2,1,0:T(8,128)(2,1)S(1)}, u32[]{:S(2)}, u32[]{:S(2)}) collective-permute-start(bf16[2,128,128]{2,1,0:T(8,128)(2,1)S(1)} %get-tuple-element.27), channel_id=1, source_target_pairs={{0,56},{8,0},{16,8},{24,16},{32,24},{40,32},{48,40},{56,48},{64,12... | collective-permute-start | bytes 196616 | tf_op jit(solution)/shard_map/ppermute | solution.py:28
  114.7 7.5 %collective-permute-start.26 = (f32[128]{0:T(128)S(1)}, f32[128]{0:T(128)S(1)}, u32[]{:S(2)}, u32[]{:S(2)}) collective-permute-start(f32[128]{0:T(128)S(1)} %bitcast.32), channel_id=1, source_target_pairs={{0,1},{1,0},{2,3},{3,2},{4,5},{5,4},{6,7},{7,6},{8,9},{9,8},{10,11... | collective-permute-start | bytes 1544 | tf_op jit(solution)/shard_map/ppermute | solution.py:328
  117.8 13.6 %collective-permute-start.25 = (bf16[8,128,128]{2,1,0:T(8,128)(2,1)S(1)}, bf16[8,128,128]{2,1,0:T(8,128)(2,1)S(1)}, u32[]{:S(2)}, u32[]{:S(2)}) collective-permute-start(bf16[8,128,128]{2,1,0:T(8,128)(2,1)S(1)} %constant_dynamic-update-slice_fusion.4.e0), channel_id=1, source_target_pairs={{0,64},{8,72},{16,80},{24,88},{32,96},{40,104},{48,112},{56,120},{... | collective-permute-start | bytes 786440 | tf_op jit(solution)/shard_map/ppermute | solution.py:28
  118.9 12.6 %collective-permute-start.24 = (bf16[8,128,128]{2,1,0:T(8,128)(2,1)S(1)}, bf16[8,128,128]{2,1,0:T(8,128)(2,1)S(1)}, u32[]{:S(2)}, u32[]{:S(2)}) collective-permute-start(bf16[8,128,128]{2,1,0:T(8,128)(2,1)S(1)} %constant_dynamic-update-slice_fusion.4.e0), channel_id=1, source_target_pairs={{0,128},{8,136},{16,144},{24,152},{32,160},{40,168},{48,176},{56,1... | collective-permute-start | bytes 786440 | tf_op jit(solution)/shard_map/ppermute | solution.py:28
  122.2 9.3 %collective-permute-start.23 = (bf16[8,128,128]{2,1,0:T(8,128)(2,1)S(1)}, bf16[8,128,128]{2,1,0:T(8,128)(2,1)S(1)}, u32[]{:S(2)}, u32[]{:S(2)}) collective-permute-start(bf16[8,128,128]{2,1,0:T(8,128)(2,1)S(1)} %constant_dynamic-update-slice_fusion.4.e0), channel_id=1, source_target_pairs={{0,192},{8,200},{16,208},{24,216},{32,224},{40,232},{48,240},{56,2... | collective-permute-start | bytes 786440 | tf_op jit(solution)/shard_map/ppermute | solution.py:28
  122.2 3.6 %collective-permute-start.27 = (f32[128]{0:T(128)S(1)}, f32[128]{0:T(128)S(1)}, u32[]{:S(2)}, u32[]{:S(2)}) collective-permute-start(f32[128]{0:T(128)S(1)} %bitcast_add_fusion), channel_id=1, source_target_pairs={{0,2},{1,3},{2,0},{3,1},{4,6},{5,7},{6,4},{7,5},{8,10},{9,11},{10,... | collective-permute-start | bytes 1544 | tf_op jit(solution)/shard_map/ppermute | solution.py:328
  125.9 5.1 %collective-permute-start.28 = (f32[128]{0:T(128)S(1)}, f32[128]{0:T(128)S(1)}, u32[]{:S(2)}, u32[]{:S(2)}) collective-permute-start(f32[128]{0:T(128)S(1)} %add.162), channel_id=1, source_target_pairs={{0,4},{1,5},{2,6},{3,7},{4,0},{5,1},{6,2},{7,3},{8,12},{9,13},{10,... | collective-permute-start | bytes 1544 | tf_op jit(solution)/shard_map/ppermute | solution.py:328

commit v3 on v2

--- a/solution.py
+++ b/solution.py
@@ -13,6 +13,7 @@
 NY = 4
 NZ = 8
 UNROLL = 8
+PAD = 8
 CHUNK = 8
 FAR = 2
 MIB = 1024 * 1024
@@ -54,11 +55,14 @@
     code = ids + col * 512 + 32768
     codes = jnp.sum(jnp.where(where[:, None] == pos[None, :], code[None, :], 0), axis=1)
     last = first + pairs
-    order = jnp.arange(max_pairs, dtype=jnp.int32)
-    owner = jnp.sum((order[:, None] >= last[None, :]).astype(jnp.int32), axis=1)
-    owner = jnp.minimum(owner, nrun - 1)
-    bounds = jnp.concatenate([first[::NZ], jnp.sum(pairs)[None]])
-    return codes.astype(jnp.int32), owner.astype(jnp.int32), bounds.astype(jnp.int32)
+    order = jnp.arange(max_pairs + PAD, dtype=jnp.int32)
+    group_start = NZ * (order - max_pairs)
+    terms = jnp.where(
+        order[:, None] < max_pairs,
+        (order[:, None] >= last[None, :]).astype(jnp.int32),
+        jnp.where(blocks[None, :] < group_start[:, None], pairs[None, :], 0),
+    )
+    return codes.astype(jnp.int32), jnp.sum(terms, axis=1).astype(jnp.int32)
 
 
 def unpack(bits_ref, masks, slot, mag):
@@ -84,8 +88,9 @@
     return jnp.concatenate(signs, axis=0), cols
 
 
-def each_pair(bounds_ref, first, last, body):
-    low, high = bounds_ref[first], bounds_ref[last]
+def each_pair(owner_ref, first, last, body):
+    base = owner_ref.shape[0] - PAD
+    low, high = owner_ref[base + first], owner_ref[base + last]
 
     def step(k, carry):
         body([low + k * UNROLL + u for u in range(UNROLL)], high)
@@ -94,16 +99,16 @@
     lax.fori_loop(0, (high - low + UNROLL - 1) // UNROLL, step, 0)
 
 
-def forward(codes_ref, owner_ref, bounds_ref, bits_ref, cur_b, groups, outs):
+def forward(codes_ref, owner_ref, bits_ref, cur_b, groups, outs):
     pl.run_scoped(
         functools.partial(
-            forward_groups, codes_ref, owner_ref, bounds_ref, bits_ref, cur_b, groups, outs
+            forward_groups, codes_ref, owner_ref, bits_ref, cur_b, groups, outs
         ),
         pltpu.VMEM((NZ, B, B), jnp.float32),
     )
 
 
-def forward_groups(codes_ref, owner_ref, bounds_ref, bits_ref, cur_b, groups, outs, total):
+def forward_groups(codes_ref, owner_ref, bits_ref, cur_b, groups, outs, total):
     masks = bit_masks()
     for group, out in zip(groups, outs):
         total[...] = jnp.zeros_like(total)
@@ -120,11 +125,11 @@
                 row = owner_ref[q] & (NZ - 1)
                 total[row] = total[row] + product
 
-        each_pair(bounds_ref, group, group + 1, body)
+        each_pair(owner_ref, group, group + 1, body)
         out[...] = total[...].astype(jnp.bfloat16)
 
 
-def backward(codes_ref, owner_ref, bounds_ref, bits_ref, errs, table, grad):
+def backward(codes_ref, owner_ref, bits_ref, errs, table, grad):
     masks = bit_masks()
     grad[...] = jnp.zeros_like(grad)
     for group in range(NY):
@@ -134,14 +139,14 @@
         products, places = [], []
         for q in qs:
             signs, cols = load_pair(codes_ref, bits_ref, masks, q, high)
-            row = table[owner_ref[q]]
+            row = table[owner_ref[q] & (NY * NZ - 1)]
             products.append(jnp.dot(signs, row, preferred_element_type=jnp.float32))
             places.append(cols)
         for product, cols in zip(products, places):
             for h in range(2):
                 grad[cols[h]] = grad[cols[h]] + product[h * B : (h + 1) * B]
 
-    each_pair(bounds_ref, 0, NY, body)
+    each_pair(owner_ref, 0, NY, body)
 
 
 def shrunk(cur, grad, scale, thresh):
@@ -153,7 +158,7 @@
     return ref.at[pl.ds(k * CHUNK, CHUNK)]
 
 
-def first_kernel(codes, owner, bounds, bits, w, far, cur_b, buf, sems):
+def first_kernel(codes, owner, bits, w, far, cur_b, buf, sems):
     nchunks = w.shape[0] // CHUNK
     for k in range(nchunks):
         pltpu.make_async_copy(chunk(w, k), chunk(buf, k), sems.at[k]).start()
@@ -166,16 +171,16 @@
         return carry
 
     lax.fori_loop(0, nchunks, turn, 0)
-    forward(codes, owner, bounds, bits, cur_b, (FAR,), (far,))
+    forward(codes, owner, bits, cur_b, (FAR,), (far,))
 
 
 def middle_kernel(
-    codes, owner, bounds, step, pen, bits, e0, e1, e2, e3, w, far, cur_b, new, buf, grad, table, sem, sems
+    codes, owner, step, pen, bits, e0, e1, e2, e3, w, far, cur_b, new, buf, grad, table, sem, sems
 ):
     nchunks = w.shape[0] // CHUNK
     load = pltpu.make_async_copy(w, buf, sem)
     load.start()
-    backward(codes, owner, bounds, bits, (e0, e1, e2, e3), table, grad)
+    backward(codes, owner, bits, (e0, e1, e2, e3), table, grad)
     load.wait()
     scale = step[0] * (1.0 / 128.0)
     thresh = step[0] * pen[0]
@@ -190,7 +195,7 @@
         return carry
 
     lax.fori_loop(0, nchunks, update, 0)
-    forward(codes, owner, bounds, bits, cur_b, (FAR,), (far,))
+    forward(codes, owner, bits, cur_b, (FAR,), (far,))
     for k in range(nchunks):
         pltpu.make_async_copy(chunk(grad, k), chunk(new, k), sems.at[k]).wait()
 
@@ -202,26 +207,26 @@
         err[k] = both[k].T.astype(jnp.bfloat16)
 
 
-def near_kernel(codes, owner, bounds, bits, cur_b, p1, p3):
-    forward(codes, owner, bounds, bits, cur_b, (1, 3), (p1, p3))
-
-
-def own_kernel(codes, owner, bounds, bits, cur_b, p0):
-    forward(codes, owner, bounds, bits, cur_b, (0,), (p0,))
-
-
-def own_goal_kernel(codes, owner, bounds, bits, cur_b, margins, p0, goal):
+def near_kernel(codes, owner, bits, cur_b, p1, p3):
+    forward(codes, owner, bits, cur_b, (1, 3), (p1, p3))
+
+
+def own_kernel(codes, owner, bits, cur_b, p0):
+    forward(codes, owner, bits, cur_b, (0,), (p0,))
+
+
+def own_goal_kernel(codes, owner, bits, cur_b, margins, p0, goal):
     goal[...] = margins[...].T * 128.0
-    forward(codes, owner, bounds, bits, cur_b, (0,), (p0,))
+    forward(codes, owner, bits, cur_b, (0,), (p0,))
 
 
 def last_kernel(
-    codes, owner, bounds, step, pen, bits, e0, e1, e2, e3, cur, out, buf, grad, table, sem, sems
+    codes, owner, step, pen, bits, e0, e1, e2, e3, cur, out, buf, grad, table, sem, sems
 ):
     nchunks = cur.shape[0] // CHUNK
     load = pltpu.make_async_copy(cur, buf, sem)
     load.start()
-    backward(codes, owner, bounds, bits, (e0, e1, e2, e3), table, grad)
+    backward(codes, owner, bits, (e0, e1, e2, e3), table, grad)
     load.wait()
     scale = step[0] * (1.0 / 128.0)
     thresh = step[0] * pen[0]
@@ -287,7 +292,10 @@
 
 def gather_runs(two):
     eight = jnp.concatenate([two, shift(two, 0, 7), shift(two, 0, 1), shift(two, 0, 6)])
-    return [eight, shift(eight, 3, 0), shift(eight, 2, 0), shift(eight, 1, 0)]
+    parts = [eight]
+    for dy in (3, 2, 1):
+        parts.append(shift(eight, dy, 0))
+    return parts
 
 
 def per_device(weights_init, margins, block_bits, run, col, tally, step_size, penalty):
@@ -324,8 +332,13 @@
     err, squares = reduce_runs(total, goal)
     errs = gather_runs(err)
     squares = squares.reshape(B)
-    for hop in (1, 2, 4):
-        squares = squares + lax.ppermute(squares, "tgt", [(k, k ^ hop) for k in range(8)])
+    squares = squares + lax.ppermute(squares, "tgt", [(k, k ^ 1) for k in range(8)])
+    others = []
+    for step in (2, 4, 6):
+        others.append(
+            lax.ppermute(squares, "tgt", [(k, (k + step) % 8) for k in range(8)])
+        )
+    squares = (squares + others[1]) + (others[0] + others[2])
     (out,) = run_kernel(
         last_kernel,
         (*lists, step_size, penalty),

time: 140 us -> 140 us (level); the launches traced: 139 us -> 138 us
  waiting for transfers between devices: 42.3 us -> 39.6 us
  starting transfers between devices: 55.9 us -> 58.3 us
    ppermute x3 -> x4, waiting for transfers between devices: 6.14 us -> 3.27 us  [the longest x3 3.26 us: per_device(): lax.ppermute(squares, 'tgt', [(k, (k + step) % 8) for k in range(8)])]
    ppermute x3 -> x4, starting transfers between devices: 2.57 us -> 5.38 us  [the longest x3 5.38 us: per_device(): lax.ppermute(squares, 'tgt', [(k, (k + step) % 8) for k in range(8)])]
  transfers between devices with their start and end apart: 29 -> 30, of which waited for: 18 -> 18; matrix products, arithmetic and copies ran while one was open for 0% -> 0% of each run, Pallas kernels for 5% -> 5%
where the time goes in v3:
time: 140 us; the launch traced here: 138 us
  starting transfers between devices  58.3 us (42%)
  waiting for transfers between devices  39.6 us (28%)
  Pallas kernels  32.1 us (23%)
  other arithmetic  3.14 us (2%)
  between operations  3.07 us (2%)
  local copies, waits for them, and re-layouts  1.43 us (1%)
    ppermute x26, starting transfers between devices, shift(): return lax.ppermute(x, 'clus', pairs)  52.9 us
    ppermute x26, waiting for transfers between devices, shift(): return lax.ppermute(x, 'clus', pairs)  36.3 us
    pallas_call x9, Pallas kernels, run_kernel(): pl.pallas_call(kernel, out_shape=[jax.ShapeDtypeStruct(s, d) for s, d in...  32.1 us
    ppermute x3, starting transfers between devices, per_device(): lax.ppermute(squares, 'tgt', [(k, (k + step) % 8) for k in range(8)])  5.38 us
    ppermute x3, waiting for transfers between devices, per_device(): lax.ppermute(squares, 'tgt', [(k, (k + step) % 8) for k in range(8)])  3.26 us
  transfers between devices with their start and end apart: 30, of which 18 were waited for; matrix products, arithmetic and copies ran while one was open for 0% of the time, Pallas kernels for 5%

profile of v3, /device:TPU:2, one launch (start us, length us, event | category | flops | bytes accessed | tf_op | source)
XLA Modules:
  0.0 137.6 jit_solution(16420448978238203174)
XLA Ops:
  1.3 0.7 fusion.13
  2.0 0.1 convert_reduce_fusion.1
  2.2 0.1 select_reduce_fusion.3
  2.4 0.2 convert_reduce_fusion
  2.6 0.7 add_add_fusion
  3.3 0.2 select_reduce_fusion.codes
  3.5 0.1 select_reduce_fusion.2.owner
  3.6 1.3 copy-done
  4.8 4.3 %shard_map.95 = (bf16[8,128,128]{2,1,0:T(8,128)(2,1)S(1)}, bf16[64,128,128]{2,1,0:T(8,128)(2,1)S(1)}) custom-call(s32[336]{0:T(512)S(1)} %select_reduce_fusion.codes, s32[176]{0:T(256)S(1)} %select_reduce_fusion.2.owner, s32[288,8,128]{2,1,0:T(8,128)S(1)} %bitcast.24, f32[64,128,128]{2,1,0:T(8,128)} %bitcast.32), custom_call_target="tpu_custom_call" | custom-call | flops 2684354560 | bytes 4194304 | tf_op jit(solution)/shard_map/pallas_call | solution.py:252
  9.2 2.9 %collective-permute-start = (bf16[8,128,128]{2,1,0:T(8,128)(2,1)S(1)}, bf16[8,128,128]{2,1,0:T(8,128)(2,1)S(1)}, u32[]{:S(2)}, u32[]{:S(2)}) collective-permute-start(bf16[8,128,128]{2,1,0:T(8,128)(2,1)S(1)} %get-tuple-element.18), channel_id=1, source_target_pairs={{0,128},{8,136},{16,144},{24,152},{32,160},{40,168},{48,176},{56,1... | collective-permute-start | bytes 786440 | tf_op jit(solution)/shard_map/ppermute | solution.py:29
  12.1 3.4 %shard_map.97 = (bf16[8,128,128]{2,1,0:T(8,128)(2,1)S(1)}, bf16[8,128,128]{2,1,0:T(8,128)(2,1)S(1)}) custom-call(s32[336]{0:T(512)S(1)} %select_reduce_fusion.codes, s32[176]{0:T(256)S(1)} %select_reduce_fusion.2.owner, s32[288,8,128]{2,1,0:T(8,128)S(1)} %bitcast.25, bf16[64,128,128]{2,1,0:T(8,128)(2,1)S(1)} %get-tuple-element.16.cur_b), custom_call_target="tpu_custom_call" | custom-call | flops 2684354560 | bytes 4194304 | tf_op jit(solution)/shard_map/pallas_call | solution.py:252
  15.5 0.7 collective-permute-start.1
  16.3 2.6 %collective-permute-start.2 = (bf16[8,128,128]{2,1,0:T(8,128)(2,1)S(1)}, bf16[8,128,128]{2,1,0:T(8,128)(2,1)S(1)}, u32[]{:S(2)}, u32[]{:S(2)}) collective-permute-start(bf16[8,128,128]{2,1,0:T(8,128)(2,1)S(1)} %get-tuple-element.20), channel_id=1, source_target_pairs={{0,192},{8,200},{16,208},{24,216},{32,224},{40,232},{48,240},{56,2... | collective-permute-start | bytes 786440 | tf_op jit(solution)/shard_map/ppermute | solution.py:29
  18.9 2.1 %shard_map.96 = (bf16[8,128,128]{2,1,0:T(8,128)(2,1)S(1)}, f32[128,128]{1,0:T(8,128)S(1)}) custom-call(s32[336]{0:T(512)S(1)} %select_reduce_fusion.codes, s32[176]{0:T(256)S(1)} %select_reduce_fusion.2.owner, s32[288,8,128]{2,1,0:T(8,128)S(1)} %bitcast.26, bf16[64,128,128]{2,1,0:T(8,128)(2,1)S(1)} %get-tuple-element.16.cur_b, f32[128,128]{1,0:T(8,128)S(1)} %copy-done.2), custom_call_target="tpu_custom_call" | custom-call | flops 1342177280 | bytes 4194304 | tf_op jit(solution)/shard_map/pallas_call | solution.py:252
  21.0 3.6 %collective-permute-done.1 = bf16[8,128,128]{2,1,0:T(8,128)(2,1)S(1)} collective-permute-done((bf16[8,128,128]{2,1,0:T(8,128)(2,1)S(1)}, bf16[8,128,128]{2,1,0:T(8,128)(2,1)S(1)}, u32[]{:S(2)}, u32[]{:S(2)}) %collective-permute-start.1) | collective-permute-done | bytes 262176 | tf_op jit(solution)/shard_map/ppermute | solution.py:29
  24.6 0.2 collective-permute-done.2
  24.8 0.1 fusion.18
  25.0 3.2 %collective-permute-start.3 = (bf16[2,128,128]{2,1,0:T(8,128)(2,1)S(1)}, bf16[2,128,128]{2,1,0:T(8,128)(2,1)S(1)}, u32[]{:S(2)}, u32[]{:S(2)}) collective-permute-start(bf16[2,128,128]{2,1,0:T(8,128)(2,1)S(1)} %get-tuple-element.37), channel_id=1, source_target_pairs={{0,16},{8,24},{16,32},{24,40},{32,48},{40,56},{48,0},{56,8},{64,80... | collective-permute-start | bytes 196616 | tf_op jit(solution)/shard_map/ppermute | solution.py:29
  28.2 2.9 %collective-permute-start.5 = (bf16[2,128,128]{2,1,0:T(8,128)(2,1)S(1)}, bf16[2,128,128]{2,1,0:T(8,128)(2,1)S(1)}, u32[]{:S(2)}, u32[]{:S(2)}) collective-permute-start(bf16[2,128,128]{2,1,0:T(8,128)(2,1)S(1)} %get-tuple-element.38), channel_id=1, source_target_pairs={{0,56},{8,0},{16,8},{24,16},{32,24},{40,32},{48,40},{56,48},{64,12... | collective-permute-start | bytes 196616 | tf_op jit(solution)/shard_map/ppermute | solution.py:29
  31.1 4.8 %collective-permute-done.3 = bf16[2,128,128]{2,1,0:T(8,128)(2,1)S(1)} collective-permute-done((bf16[2,128,128]{2,1,0:T(8,128)(2,1)S(1)}, bf16[2,128,128]{2,1,0:T(8,128)(2,1)S(1)}, u32[]{:S(2)}, u32[]{:S(2)}) %collective-permute-start.3) | collective-permute-done | bytes 65568 | tf_op jit(solution)/shard_map/ppermute | solution.py:29
  35.9 0.7 collective-permute-done.4
  36.7 5.7 %collective-permute-start.6 = (bf16[2,128,128]{2,1,0:T(8,128)(2,1)S(1)}, bf16[2,128,128]{2,1,0:T(8,128)(2,1)S(1)}, u32[]{:S(2)}, u32[]{:S(2)}) collective-permute-start(bf16[2,128,128]{2,1,0:T(8,128)(2,1)S(1)} %rev.12), channel_id=1, source_target_pairs={{0,32},{8,40},{16,48},{24,56},{32,0},{40,8},{48,16},{56,24},{64,96... | collective-permute-start | bytes 196616 | tf_op jit(solution)/shard_map/ppermute | solution.py:29
  42.4 2.8 %collective-permute-done.6.other = bf16[2,128,128]{2,1,0:T(8,128)(2,1)S(1)} collective-permute-done((bf16[2,128,128]{2,1,0:T(8,128)(2,1)S(1)}, bf16[2,128,128]{2,1,0:T(8,128)(2,1)S(1)}, u32[]{:S(2)}, u32[]{:S(2)}) %collective-permute-start.6) | collective-permute-done | bytes 65568 | tf_op jit(solution)/shard_map/ppermute | solution.py:29
  45.2 0.5 shard_map.98
  45.8 2.9 %collective-permute-start.9 = (bf16[2,128,128]{2,1,0:T(8,128)(2,1)S(1)}, bf16[2,128,128]{2,1,0:T(8,128)(2,1)S(1)}, u32[]{:S(2)}, u32[]{:S(2)}) collective-permute-start(bf16[2,128,128]{2,1,0:T(8,128)(2,1)S(1)} %get-tuple-element.22), channel_id=1, source_target_pairs={{0,48},{8,56},{16,0},{24,8},{32,16},{40,24},{48,32},{56,40},{64,11... | collective-permute-start | bytes 196616 | tf_op jit(solution)/shard_map/ppermute | solution.py:29
  48.7 3.2 %collective-permute-start.7 = (bf16[2,128,128]{2,1,0:T(8,128)(2,1)S(1)}, bf16[2,128,128]{2,1,0:T(8,128)(2,1)S(1)}, u32[]{:S(2)}, u32[]{:S(2)}) collective-permute-start(bf16[2,128,128]{2,1,0:T(8,128)(2,1)S(1)} %get-tuple-element.22), channel_id=1, source_target_pairs={{0,56},{8,0},{16,8},{24,16},{32,24},{40,32},{48,40},{56,48},{64,12... | collective-permute-start | bytes 196616 | tf_op jit(solution)/shard_map/ppermute | solution.py:29
  51.9 1.9 %collective-permute-done.7 = bf16[2,128,128]{2,1,0:T(8,128)(2,1)S(1)} collective-permute-done((bf16[2,128,128]{2,1,0:T(8,128)(2,1)S(1)}, bf16[2,128,128]{2,1,0:T(8,128)(2,1)S(1)}, u32[]{:S(2)}, u32[]{:S(2)}) %collective-permute-start.7) | collective-permute-done | bytes 65568 | tf_op jit(solution)/shard_map/ppermute | solution.py:29
  53.8 0.3 collective-permute-done.8
  54.2 1.0 collective-permute-start.12
  55.2 3.5 %collective-permute-start.11 = (bf16[8,128,128]{2,1,0:T(8,128)(2,1)S(1)}, bf16[8,128,128]{2,1,0:T(8,128)(2,1)S(1)}, u32[]{:S(2)}, u32[]{:S(2)}) collective-permute-start(bf16[8,128,128]{2,1,0:T(8,128)(2,1)S(1)} %constant_dynamic-update-slice_fusion.e0), channel_id=1, source_target_pairs={{0,128},{8,136},{16,144},{24,152},{32,160},{40,168},{48,176},{56,1... | collective-permute-start | bytes 786440 | tf_op jit(solution)/shard_map/ppermute | solution.py:29
  58.7 0.3 collective-permute-start.10
  60.3 3.1 %collective-permute-done.12.e3 = bf16[8,128,128]{2,1,0:T(8,128)(2,1)S(1)} collective-permute-done((bf16[8,128,128]{2,1,0:T(8,128)(2,1)S(1)}, bf16[8,128,128]{2,1,0:T(8,128)(2,1)S(1)}, u32[]{:S(2)}, u32[]{:S(2)}) %collective-permute-start.12) | collective-permute-done | bytes 262176 | tf_op jit(solution)/shard_map/ppermute | solution.py:29
  63.4 2.8 %collective-permute-done.11.e2 = bf16[8,128,128]{2,1,0:T(8,128)(2,1)S(1)} collective-permute-done((bf16[8,128,128]{2,1,0:T(8,128)(2,1)S(1)}, bf16[8,128,128]{2,1,0:T(8,128)(2,1)S(1)}, u32[]{:S(2)}, u32[]{:S(2)}) %collective-permute-start.11) | collective-permute-done | bytes 262176 | tf_op jit(solution)/shard_map/ppermute | solution.py:29
  66.2 8.4 %shard_map.99 = (bf16[8,128,128]{2,1,0:T(8,128)(2,1)S(1)}, bf16[64,128,128]{2,1,0:T(8,128)(2,1)S(1)}, f32[64,128,128]{2,1,0:T(8,128)}) custom-call(s32[336]{0:T(512)S(1)} %select_reduce_fusion.codes, s32[176]{0:T(256)S(1)} %select_reduce_fusion.2.owner, f32[1]{0:T(128)S(6)} %copy.17.step, f32[1]{0:T(128)S(6)} %copy.18.pen, s32[288,8,128]{2,1,0:T(8,128)S(1)} %bitcast.27, ...), custom_call_target="tpu_custom_call" | custom-call | flops 8053063680 | bytes 4194304 | tf_op jit(solution)/shard_map/pallas_call | solution.py:252
  74.6 3.4 %shard_map.101 = (bf16[8,128,128]{2,1,0:T(8,128)(2,1)S(1)}, bf16[8,128,128]{2,1,0:T(8,128)(2,1)S(1)}) custom-call(s32[336]{0:T(512)S(1)} %select_reduce_fusion.codes, s32[176]{0:T(256)S(1)} %select_reduce_fusion.2.owner, s32[288,8,128]{2,1,0:T(8,128)S(1)} %bitcast.28, bf16[64,128,128]{2,1,0:T(8,128)(2,1)S(1)} %get-tuple-element.23.cur_b), custom_call_target="tpu_custom_call" | custom-call | flops 2684354560 | bytes 4194304 | tf_op jit(solution)/shard_map/pallas_call | solution.py:252
  78.0 0.8 collective-permute-start.14
  78.8 4.0 %collective-permute-start.15 = (bf16[8,128,128]{2,1,0:T(8,128)(2,1)S(1)}, bf16[8,128,128]{2,1,0:T(8,128)(2,1)S(1)}, u32[]{:S(2)}, u32[]{:S(2)}) collective-permute-start(bf16[8,128,128]{2,1,0:T(8,128)(2,1)S(1)} %get-tuple-element.26), channel_id=1, source_target_pairs={{0,192},{8,200},{16,208},{24,216},{32,224},{40,232},{48,240},{56,2... | collective-permute-start | bytes 786440 | tf_op jit(solution)/shard_map/ppermute | solution.py:29
  82.8 1.4 collective-permute-start.13
  84.2 2.0 %shard_map.100 = bf16[8,128,128]{2,1,0:T(8,128)(2,1)S(1)} custom-call(s32[336]{0:T(512)S(1)} %select_reduce_fusion.codes, s32[176]{0:T(256)S(1)} %select_reduce_fusion.2.owner, s32[288,8,128]{2,1,0:T(8,128)S(1)} %bitcast.29, bf16[64,128,128]{2,1,0:T(8,128)(2,1)S(1)} %get-tuple-element.23.cur_b), custom_call_target="tpu_custom_call" | custom-call | flops 1342177280 | bytes 4194304 | tf_op jit(solution)/shard_map/pallas_call | solution.py:252
  86.2 2.9 %collective-permute-done.14 = bf16[8,128,128]{2,1,0:T(8,128)(2,1)S(1)} collective-permute-done((bf16[8,128,128]{2,1,0:T(8,128)(2,1)S(1)}, bf16[8,128,128]{2,1,0:T(8,128)(2,1)S(1)}, u32[]{:S(2)}, u32[]{:S(2)}) %collective-permute-start.14) | collective-permute-done | bytes 262176 | tf_op jit(solution)/shard_map/ppermute | solution.py:29
  89.2 1.1 collective-permute-done.15
  90.3 1.7 %collective-permute-done.13 = bf16[8,128,128]{2,1,0:T(8,128)(2,1)S(1)} collective-permute-done((bf16[8,128,128]{2,1,0:T(8,128)(2,1)S(1)}, bf16[8,128,128]{2,1,0:T(8,128)(2,1)S(1)}, u32[]{:S(2)}, u32[]{:S(2)}) %collective-permute-start.13) | collective-permute-done | bytes 262176 | tf_op jit(solution)/shard_map/ppermute | solution.py:29
  92.0 0.1 fusion.17
  92.2 1.5 %collective-permute-start.18 = (bf16[2,128,128]{2,1,0:T(8,128)(2,1)S(1)}, bf16[2,128,128]{2,1,0:T(8,128)(2,1)S(1)}, u32[]{:S(2)}, u32[]{:S(2)}) collective-permute-start(bf16[2,128,128]{2,1,0:T(8,128)(2,1)S(1)} %get-tuple-element.35), channel_id=1, source_target_pairs={{0,56},{8,0},{16,8},{24,16},{32,24},{40,32},{48,40},{56,48},{64,12... | collective-permute-start | bytes 196616 | tf_op jit(solution)/shard_map/ppermute | solution.py:29
  93.7 2.2 %collective-permute-start.17 = (bf16[2,128,128]{2,1,0:T(8,128)(2,1)S(1)}, bf16[2,128,128]{2,1,0:T(8,128)(2,1)S(1)}, u32[]{:S(2)}, u32[]{:S(2)}) collective-permute-start(bf16[2,128,128]{2,1,0:T(8,128)(2,1)S(1)} %get-tuple-element.36), channel_id=1, source_target_pairs={{0,8},{8,16},{16,24},{24,32},{32,40},{40,48},{48,56},{56,0},{64,72... | collective-permute-start | bytes 196616 | tf_op jit(solution)/shard_map/ppermute | solution.py:29
  95.9 3.3 %collective-permute-done.16 = bf16[2,128,128]{2,1,0:T(8,128)(2,1)S(1)} collective-permute-done((bf16[2,128,128]{2,1,0:T(8,128)(2,1)S(1)}, bf16[2,128,128]{2,1,0:T(8,128)(2,1)S(1)}, u32[]{:S(2)}, u32[]{:S(2)}) %collective-permute-start.16) | collective-permute-done | bytes 65568 | tf_op jit(solution)/shard_map/ppermute | solution.py:29
  99.3 0.2 collective-permute-done.17
  99.6 4.7 %collective-permute-start.19 = (bf16[2,128,128]{2,1,0:T(8,128)(2,1)S(1)}, bf16[2,128,128]{2,1,0:T(8,128)(2,1)S(1)}, u32[]{:S(2)}, u32[]{:S(2)}) collective-permute-start(bf16[2,128,128]{2,1,0:T(8,128)(2,1)S(1)} %rev.11), channel_id=1, source_target_pairs={{0,32},{8,40},{16,48},{24,56},{32,0},{40,8},{48,16},{56,24},{64,96... | collective-permute-start | bytes 196616 | tf_op jit(solution)/shard_map/ppermute | solution.py:29
  104.2 3.7 %collective-permute-done.19.other = bf16[2,128,128]{2,1,0:T(8,128)(2,1)S(1)} collective-permute-done((bf16[2,128,128]{2,1,0:T(8,128)(2,1)S(1)}, bf16[2,128,128]{2,1,0:T(8,128)(2,1)S(1)}, u32[]{:S(2)}, u32[]{:S(2)}) %collective-permute-start.19) | collective-permute-done | bytes 65568 | tf_op jit(solution)/shard_map/ppermute | solution.py:29
  108.0 0.1 shard_map.102
  108.1 1.9 %collective-permute-start.22 = (bf16[2,128,128]{2,1,0:T(8,128)(2,1)S(1)}, bf16[2,128,128]{2,1,0:T(8,128)(2,1)S(1)}, u32[]{:S(2)}, u32[]{:S(2)}) collective-permute-start(bf16[2,128,128]{2,1,0:T(8,128)(2,1)S(1)} %get-tuple-element.27), channel_id=1, source_target_pairs={{0,48},{8,56},{16,0},{24,8},{32,16},{40,24},{48,32},{56,40},{64,11... | collective-permute-start | bytes 196616 | tf_op jit(solution)/shard_map/ppermute | solution.py:29
  110.0 2.1 %collective-permute-start.21 = (bf16[2,128,128]{2,1,0:T(8,128)(2,1)S(1)}, bf16[2,128,128]{2,1,0:T(8,128)(2,1)S(1)}, u32[]{:S(2)}, u32[]{:S(2)}) collective-permute-start(bf16[2,128,128]{2,1,0:T(8,128)(2,1)S(1)} %get-tuple-element.27), channel_id=1, source_target_pairs={{0,8},{8,16},{16,24},{24,32},{32,40},{40,48},{48,56},{56,0},{64,72... | collective-permute-start | bytes 196616 | tf_op jit(solution)/shard_map/ppermute | solution.py:29
  112.0 1.2 collective-permute-start.20
  113.2 3.1 %collective-permute-done.20 = bf16[2,128,128]{2,1,0:T(8,128)(2,1)S(1)} collective-permute-done((bf16[2,128,128]{2,1,0:T(8,128)(2,1)S(1)}, bf16[2,128,128]{2,1,0:T(8,128)(2,1)S(1)}, u32[]{:S(2)}, u32[]{:S(2)}) %collective-permute-start.20) | collective-permute-done | bytes 65568 | tf_op jit(solution)/shard_map/ppermute | solution.py:29
  116.4 1.1 collective-permute-start.25
  117.4 2.0 %collective-permute-start.24 = (bf16[8,128,128]{2,1,0:T(8,128)(2,1)S(1)}, bf16[8,128,128]{2,1,0:T(8,128)(2,1)S(1)}, u32[]{:S(2)}, u32[]{:S(2)}) collective-permute-start(bf16[8,128,128]{2,1,0:T(8,128)(2,1)S(1)} %constant_dynamic-update-slice_fusion.4.e0), channel_id=1, source_target_pairs={{0,128},{8,136},{16,144},{24,152},{32,160},{40,168},{48,176},{56,1... | collective-permute-start | bytes 786440 | tf_op jit(solution)/shard_map/ppermute | solution.py:29
  119.5 1.0 collective-permute-start.23
  120.5 0.8 collective-permute-start.29
  121.2 1.2 collective-permute-start.28
  122.5 1.5 %collective-permute-done.29 = f32[128]{0:T(128)S(1)} collective-permute-done((f32[128]{0:T(128)S(1)}, f32[128]{0:T(128)S(1)}, u32[]{:S(2)}, u32[]{:S(2)}) %collective-permute-start.29) | collective-permute-done | bytes 544 | tf_op jit(solution)/shard_map/ppermute | solution.py:339
  124.0 3.3 %collective-permute-start.27 = (f32[128]{0:T(128)S(1)}, f32[128]{0:T(128)S(1)}, u32[]{:S(2)}, u32[]{:S(2)}) collective-permute-start(f32[128]{0:T(128)S(1)} %bitcast_add_fusion), channel_id=1, source_target_pairs={{0,4},{1,5},{2,6},{3,7},{4,0},{5,1},{6,2},{7,3},{8,12},{9,13},{10,... | collective-permute-start | bytes 1544 | tf_op jit(solution)/shard_map/ppermute | solution.py:339
  127.4 1.7 %collective-permute-done.27 = f32[128]{0:T(128)S(1)} collective-permute-done((f32[128]{0:T(128)S(1)}, f32[128]{0:T(128)S(1)}, u32[]{:S(2)}, u32[]{:S(2)}) %collective-permute-start.27) | collective-permute-done | bytes 544 | tf_op jit(solution)/shard_map/ppermute | solution.py:339
  129.1 0.5 add_multiply_fusion.1
  129.6 7.8 %shard_map.103 = f32[64,128,128]{2,1,0:T(8,128)} custom-call(s32[336]{0:T(512)S(1)} %select_reduce_fusion.codes, s32[176]{0:T(256)S(1)} %select_reduce_fusion.2.owner, f32[1]{0:T(128)S(6)} %copy.17.step, f32[1]{0:T(128)S(6)} %copy.18.pen, s32[288,8,128]{2,1,0:T(8,128)S(1)} %bitcast.30, bf16[8,128,128]{2,1,0:T(8,128)(2,1)S(1)} %constant_dynamic-update-slice_fusion.4.e0, ...), custom_call_target="tpu_custom_call" | custom-call | flops 6710886400 | bytes 4194304 | tf_op jit(solution)/shard_map/pallas_call | solution.py:252
  (47 shorter events, 0.6 us)
Async XLA Ops:
  3.6 1.3 copy-start
  9.2 11.8 %collective-permute-start = (bf16[8,128,128]{2,1,0:T(8,128)(2,1)S(1)}, bf16[8,128,128]{2,1,0:T(8,128)(2,1)S(1)}, u32[]{:S(2)}, u32[]{:S(2)}) collective-permute-start(bf16[8,128,128]{2,1,0:T(8,128)(2,1)S(1)} %get-tuple-element.18), channel_id=1, source_target_pairs={{0,128},{8,136},{16,144},{24,152},{32,160},{40,168},{48,176},{56,1... | collective-permute-start | bytes 786440 | tf_op jit(solution)/shard_map/ppermute | solution.py:29
  12.1 6.8 %copy-start.2 = (f32[128,128]{1,0:T(8,128)S(1)}, f32[128,128]{1,0:T(8,128)}, u32[]{:S(2)}) copy-start(f32[128,128]{1,0:T(8,128)} %margins.1) | copy-start | bytes 196612
  15.5 9.1 %collective-permute-start.1 = (bf16[8,128,128]{2,1,0:T(8,128)(2,1)S(1)}, bf16[8,128,128]{2,1,0:T(8,128)(2,1)S(1)}, u32[]{:S(2)}, u32[]{:S(2)}) collective-permute-start(bf16[8,128,128]{2,1,0:T(8,128)(2,1)S(1)} %get-tuple-element.19), channel_id=1, source_target_pairs={{0,64},{8,72},{16,80},{24,88},{32,96},{40,104},{48,112},{56,120},{... | collective-permute-start | bytes 786440 | tf_op jit(solution)/shard_map/ppermute | solution.py:29
  16.3 49.9 %copy-start.1 = (s32[288,128,8]{1,2,0:T(8,128)S(1)}, s32[288,128,8]{1,2,0:T(8,128)}, u32[]{:S(2)}) copy-start(s32[288,128,8]{1,2,0:T(8,128)} %param.10) | copy-start | bytes 3538948
  16.3 8.5 %collective-permute-start.2 = (bf16[8,128,128]{2,1,0:T(8,128)(2,1)S(1)}, bf16[8,128,128]{2,1,0:T(8,128)(2,1)S(1)}, u32[]{:S(2)}, u32[]{:S(2)}) collective-permute-start(bf16[8,128,128]{2,1,0:T(8,128)(2,1)S(1)} %get-tuple-element.20), channel_id=1, source_target_pairs={{0,192},{8,200},{16,208},{24,216},{32,224},{40,232},{48,240},{56,2... | collective-permute-start | bytes 786440 | tf_op jit(solution)/shard_map/ppermute | solution.py:29
  25.0 10.9 %collective-permute-start.3 = (bf16[2,128,128]{2,1,0:T(8,128)(2,1)S(1)}, bf16[2,128,128]{2,1,0:T(8,128)(2,1)S(1)}, u32[]{:S(2)}, u32[]{:S(2)}) collective-permute-start(bf16[2,128,128]{2,1,0:T(8,128)(2,1)S(1)} %get-tuple-element.37), channel_id=1, source_target_pairs={{0,16},{8,24},{16,32},{24,40},{32,48},{40,56},{48,0},{56,8},{64,80... | collective-permute-start | bytes 196616 | tf_op jit(solution)/shard_map/ppermute | solution.py:29
  28.2 7.7 %collective-permute-start.5 = (bf16[2,128,128]{2,1,0:T(8,128)(2,1)S(1)}, bf16[2,128,128]{2,1,0:T(8,128)(2,1)S(1)}, u32[]{:S(2)}, u32[]{:S(2)}) collective-permute-start(bf16[2,128,128]{2,1,0:T(8,128)(2,1)S(1)} %get-tuple-element.38), channel_id=1, source_target_pairs={{0,56},{8,0},{16,8},{24,16},{32,24},{40,32},{48,40},{56,48},{64,12... | collective-permute-start | bytes 196616 | tf_op jit(solution)/shard_map/ppermute | solution.py:29
  31.1 5.5 %collective-permute-start.4 = (bf16[2,128,128]{2,1,0:T(8,128)(2,1)S(1)}, bf16[2,128,128]{2,1,0:T(8,128)(2,1)S(1)}, u32[]{:S(2)}, u32[]{:S(2)}) collective-permute-start(bf16[2,128,128]{2,1,0:T(8,128)(2,1)S(1)} %get-tuple-element.39), channel_id=1, source_target_pairs={{0,8},{8,16},{16,24},{24,32},{32,40},{40,48},{48,56},{56,0},{64,72... | collective-permute-start | bytes 196616 | tf_op jit(solution)/shard_map/ppermute | solution.py:29
  36.7 8.5 %collective-permute-start.6 = (bf16[2,128,128]{2,1,0:T(8,128)(2,1)S(1)}, bf16[2,128,128]{2,1,0:T(8,128)(2,1)S(1)}, u32[]{:S(2)}, u32[]{:S(2)}) collective-permute-start(bf16[2,128,128]{2,1,0:T(8,128)(2,1)S(1)} %rev.12), channel_id=1, source_target_pairs={{0,32},{8,40},{16,48},{24,56},{32,0},{40,8},{48,16},{56,24},{64,96... | collective-permute-start | bytes 196616 | tf_op jit(solution)/shard_map/ppermute | solution.py:29
  45.8 8.4 %collective-permute-start.9 = (bf16[2,128,128]{2,1,0:T(8,128)(2,1)S(1)}, bf16[2,128,128]{2,1,0:T(8,128)(2,1)S(1)}, u32[]{:S(2)}, u32[]{:S(2)}) collective-permute-start(bf16[2,128,128]{2,1,0:T(8,128)(2,1)S(1)} %get-tuple-element.22), channel_id=1, source_target_pairs={{0,48},{8,56},{16,0},{24,8},{32,16},{40,24},{48,32},{56,40},{64,11... | collective-permute-start | bytes 196616 | tf_op jit(solution)/shard_map/ppermute | solution.py:29
  48.7 5.5 %collective-permute-start.8 = (bf16[2,128,128]{2,1,0:T(8,128)(2,1)S(1)}, bf16[2,128,128]{2,1,0:T(8,128)(2,1)S(1)}, u32[]{:S(2)}, u32[]{:S(2)}) collective-permute-start(bf16[2,128,128]{2,1,0:T(8,128)(2,1)S(1)} %get-tuple-element.22), channel_id=1, source_target_pairs={{0,8},{8,16},{16,24},{24,32},{32,40},{40,48},{48,56},{56,0},{64,72... | collective-permute-start | bytes 196616 | tf_op jit(solution)/shard_map/ppermute | solution.py:29
  48.7 5.1 %collective-permute-start.7 = (bf16[2,128,128]{2,1,0:T(8,128)(2,1)S(1)}, bf16[2,128,128]{2,1,0:T(8,128)(2,1)S(1)}, u32[]{:S(2)}, u32[]{:S(2)}) collective-permute-start(bf16[2,128,128]{2,1,0:T(8,128)(2,1)S(1)} %get-tuple-element.22), channel_id=1, source_target_pairs={{0,56},{8,0},{16,8},{24,16},{32,24},{40,32},{48,40},{56,48},{64,12... | collective-permute-start | bytes 196616 | tf_op jit(solution)/shard_map/ppermute | solution.py:29
  54.2 9.2 %collective-permute-start.12 = (bf16[8,128,128]{2,1,0:T(8,128)(2,1)S(1)}, bf16[8,128,128]{2,1,0:T(8,128)(2,1)S(1)}, u32[]{:S(2)}, u32[]{:S(2)}) collective-permute-start(bf16[8,128,128]{2,1,0:T(8,128)(2,1)S(1)} %constant_dynamic-update-slice_fusion.e0), channel_id=1, source_target_pairs={{0,64},{8,72},{16,80},{24,88},{32,96},{40,104},{48,112},{56,120},{... | collective-permute-start | bytes 786440 | tf_op jit(solution)/shard_map/ppermute | solution.py:29
  55.2 11.0 %collective-permute-start.11 = (bf16[8,128,128]{2,1,0:T(8,128)(2,1)S(1)}, bf16[8,128,128]{2,1,0:T(8,128)(2,1)S(1)}, u32[]{:S(2)}, u32[]{:S(2)}) collective-permute-start(bf16[8,128,128]{2,1,0:T(8,128)(2,1)S(1)} %constant_dynamic-update-slice_fusion.e0), channel_id=1, source_target_pairs={{0,128},{8,136},{16,144},{24,152},{32,160},{40,168},{48,176},{56,1... | collective-permute-start | bytes 786440 | tf_op jit(solution)/shard_map/ppermute | solution.py:29
  58.7 7.5 %collective-permute-start.10 = (bf16[8,128,128]{2,1,0:T(8,128)(2,1)S(1)}, bf16[8,128,128]{2,1,0:T(8,128)(2,1)S(1)}, u32[]{:S(2)}, u32[]{:S(2)}) collective-permute-start(bf16[8,128,128]{2,1,0:T(8,128)(2,1)S(1)} %constant_dynamic-update-slice_fusion.e0), channel_id=1, source_target_pairs={{0,192},{8,200},{16,208},{24,216},{32,224},{40,232},{48,240},{56,2... | collective-permute-start | bytes 786440 | tf_op jit(solution)/shard_map/ppermute | solution.py:29
  78.0 11.2 %collective-permute-start.14 = (bf16[8,128,128]{2,1,0:T(8,128)(2,1)S(1)}, bf16[8,128,128]{2,1,0:T(8,128)(2,1)S(1)}, u32[]{:S(2)}, u32[]{:S(2)}) collective-permute-start(bf16[8,128,128]{2,1,0:T(8,128)(2,1)S(1)} %get-tuple-element.25), channel_id=1, source_target_pairs={{0,64},{8,72},{16,80},{24,88},{32,96},{40,104},{48,112},{56,120},{... | collective-permute-start | bytes 786440 | tf_op jit(solution)/shard_map/ppermute | solution.py:29
  78.8 11.4 %collective-permute-start.15 = (bf16[8,128,128]{2,1,0:T(8,128)(2,1)S(1)}, bf16[8,128,128]{2,1,0:T(8,128)(2,1)S(1)}, u32[]{:S(2)}, u32[]{:S(2)}) collective-permute-start(bf16[8,128,128]{2,1,0:T(8,128)(2,1)S(1)} %get-tuple-element.26), channel_id=1, source_target_pairs={{0,192},{8,200},{16,208},{24,216},{32,224},{40,232},{48,240},{56,2... | collective-permute-start | bytes 786440 | tf_op jit(solution)/shard_map/ppermute | solution.py:29
  82.8 9.1 %collective-permute-start.13 = (bf16[8,128,128]{2,1,0:T(8,128)(2,1)S(1)}, bf16[8,128,128]{2,1,0:T(8,128)(2,1)S(1)}, u32[]{:S(2)}, u32[]{:S(2)}) collective-permute-start(bf16[8,128,128]{2,1,0:T(8,128)(2,1)S(1)} %get-tuple-element.24), channel_id=1, source_target_pairs={{0,128},{8,136},{16,144},{24,152},{32,160},{40,168},{48,176},{56,1... | collective-permute-start | bytes 786440 | tf_op jit(solution)/shard_map/ppermute | solution.py:29
  92.2 7.1 %collective-permute-start.16 = (bf16[2,128,128]{2,1,0:T(8,128)(2,1)S(1)}, bf16[2,128,128]{2,1,0:T(8,128)(2,1)S(1)}, u32[]{:S(2)}, u32[]{:S(2)}) collective-permute-start(bf16[2,128,128]{2,1,0:T(8,128)(2,1)S(1)} %get-tuple-element.34), channel_id=1, source_target_pairs={{0,16},{8,24},{16,32},{24,40},{32,48},{40,56},{48,0},{56,8},{64,80... | collective-permute-start | bytes 196616 | tf_op jit(solution)/shard_map/ppermute | solution.py:29
  92.2 7.0 %collective-permute-start.18 = (bf16[2,128,128]{2,1,0:T(8,128)(2,1)S(1)}, bf16[2,128,128]{2,1,0:T(8,128)(2,1)S(1)}, u32[]{:S(2)}, u32[]{:S(2)}) collective-permute-start(bf16[2,128,128]{2,1,0:T(8,128)(2,1)S(1)} %get-tuple-element.35), channel_id=1, source_target_pairs={{0,56},{8,0},{16,8},{24,16},{32,24},{40,32},{48,40},{56,48},{64,12... | collective-permute-start | bytes 196616 | tf_op jit(solution)/shard_map/ppermute | solution.py:29
  93.7 5.7 %collective-permute-start.17 = (bf16[2,128,128]{2,1,0:T(8,128)(2,1)S(1)}, bf16[2,128,128]{2,1,0:T(8,128)(2,1)S(1)}, u32[]{:S(2)}, u32[]{:S(2)}) collective-permute-start(bf16[2,128,128]{2,1,0:T(8,128)(2,1)S(1)} %get-tuple-element.36), channel_id=1, source_target_pairs={{0,8},{8,16},{16,24},{24,32},{32,40},{40,48},{48,56},{56,0},{64,72... | collective-permute-start | bytes 196616 | tf_op jit(solution)/shard_map/ppermute | solution.py:29
  99.6 8.4 %collective-permute-start.19 = (bf16[2,128,128]{2,1,0:T(8,128)(2,1)S(1)}, bf16[2,128,128]{2,1,0:T(8,128)(2,1)S(1)}, u32[]{:S(2)}, u32[]{:S(2)}) collective-permute-start(bf16[2,128,128]{2,1,0:T(8,128)(2,1)S(1)} %rev.11), channel_id=1, source_target_pairs={{0,32},{8,40},{16,48},{24,56},{32,0},{40,8},{48,16},{56,24},{64,96... | collective-permute-start | bytes 196616 | tf_op jit(solution)/shard_map/ppermute | solution.py:29
  108.1 8.3 %collective-permute-start.22 = (bf16[2,128,128]{2,1,0:T(8,128)(2,1)S(1)}, bf16[2,128,128]{2,1,0:T(8,128)(2,1)S(1)}, u32[]{:S(2)}, u32[]{:S(2)}) collective-permute-start(bf16[2,128,128]{2,1,0:T(8,128)(2,1)S(1)} %get-tuple-element.27), channel_id=1, source_target_pairs={{0,48},{8,56},{16,0},{24,8},{32,16},{40,24},{48,32},{56,40},{64,11... | collective-permute-start | bytes 196616 | tf_op jit(solution)/shard_map/ppermute | solution.py:29
  110.0 6.3 %collective-permute-start.21 = (bf16[2,128,128]{2,1,0:T(8,128)(2,1)S(1)}, bf16[2,128,128]{2,1,0:T(8,128)(2,1)S(1)}, u32[]{:S(2)}, u32[]{:S(2)}) collective-permute-start(bf16[2,128,128]{2,1,0:T(8,128)(2,1)S(1)} %get-tuple-element.27), channel_id=1, source_target_pairs={{0,8},{8,16},{16,24},{24,32},{32,40},{40,48},{48,56},{56,0},{64,72... | collective-permute-start | bytes 196616 | tf_op jit(solution)/shard_map/ppermute | solution.py:29
  112.0 4.3 %collective-permute-start.20 = (bf16[2,128,128]{2,1,0:T(8,128)(2,1)S(1)}, bf16[2,128,128]{2,1,0:T(8,128)(2,1)S(1)}, u32[]{:S(2)}, u32[]{:S(2)}) collective-permute-start(bf16[2,128,128]{2,1,0:T(8,128)(2,1)S(1)} %get-tuple-element.27), channel_id=1, source_target_pairs={{0,56},{8,0},{16,8},{24,16},{32,24},{40,32},{48,40},{56,48},{64,12... | collective-permute-start | bytes 196616 | tf_op jit(solution)/shard_map/ppermute | solution.py:29
  113.2 7.2 %collective-permute-start.26 = (f32[128]{0:T(128)S(1)}, f32[128]{0:T(128)S(1)}, u32[]{:S(2)}, u32[]{:S(2)}) collective-permute-start(f32[128]{0:T(128)S(1)} %bitcast.31), channel_id=1, source_target_pairs={{0,1},{1,0},{2,3},{3,2},{4,5},{5,4},{6,7},{7,6},{8,9},{9,8},{10,11... | collective-permute-start | bytes 1544 | tf_op jit(solution)/shard_map/ppermute | solution.py:335
  116.4 13.3 %collective-permute-start.25 = (bf16[8,128,128]{2,1,0:T(8,128)(2,1)S(1)}, bf16[8,128,128]{2,1,0:T(8,128)(2,1)S(1)}, u32[]{:S(2)}, u32[]{:S(2)}) collective-permute-start(bf16[8,128,128]{2,1,0:T(8,128)(2,1)S(1)} %constant_dynamic-update-slice_fusion.4.e0), channel_id=1, source_target_pairs={{0,64},{8,72},{16,80},{24,88},{32,96},{40,104},{48,112},{56,120},{... | collective-permute-start | bytes 786440 | tf_op jit(solution)/shard_map/ppermute | solution.py:29
  117.4 12.2 %collective-permute-start.24 = (bf16[8,128,128]{2,1,0:T(8,128)(2,1)S(1)}, bf16[8,128,128]{2,1,0:T(8,128)(2,1)S(1)}, u32[]{:S(2)}, u32[]{:S(2)}) collective-permute-start(bf16[8,128,128]{2,1,0:T(8,128)(2,1)S(1)} %constant_dynamic-update-slice_fusion.4.e0), channel_id=1, source_target_pairs={{0,128},{8,136},{16,144},{24,152},{32,160},{40,168},{48,176},{56,1... | collective-permute-start | bytes 786440 | tf_op jit(solution)/shard_map/ppermute | solution.py:29
  119.5 10.2 %collective-permute-start.23 = (bf16[8,128,128]{2,1,0:T(8,128)(2,1)S(1)}, bf16[8,128,128]{2,1,0:T(8,128)(2,1)S(1)}, u32[]{:S(2)}, u32[]{:S(2)}) collective-permute-start(bf16[8,128,128]{2,1,0:T(8,128)(2,1)S(1)} %constant_dynamic-update-slice_fusion.4.e0), channel_id=1, source_target_pairs={{0,192},{8,200},{16,208},{24,216},{32,224},{40,232},{48,240},{56,2... | collective-permute-start | bytes 786440 | tf_op jit(solution)/shard_map/ppermute | solution.py:29
  120.5 3.6 %collective-permute-start.29 = (f32[128]{0:T(128)S(1)}, f32[128]{0:T(128)S(1)}, u32[]{:S(2)}, u32[]{:S(2)}) collective-permute-start(f32[128]{0:T(128)S(1)} %bitcast_add_fusion), channel_id=1, source_target_pairs={{0,6},{1,7},{2,0},{3,1},{4,2},{5,3},{6,4},{7,5},{8,14},{9,15},{10,... | collective-permute-start | bytes 1544 | tf_op jit(solution)/shard_map/ppermute | solution.py:339
  121.2 6.1 %collective-permute-start.28 = (f32[128]{0:T(128)S(1)}, f32[128]{0:T(128)S(1)}, u32[]{:S(2)}, u32[]{:S(2)}) collective-permute-start(f32[128]{0:T(128)S(1)} %bitcast_add_fusion), channel_id=1, source_target_pairs={{0,2},{1,3},{2,4},{3,5},{4,6},{5,7},{6,0},{7,1},{8,10},{9,11},{10,... | collective-permute-start | bytes 1544 | tf_op jit(solution)/shard_map/ppermute | solution.py:339
  124.0 5.1 %collective-permute-start.27 = (f32[128]{0:T(128)S(1)}, f32[128]{0:T(128)S(1)}, u32[]{:S(2)}, u32[]{:S(2)}) collective-permute-start(f32[128]{0:T(128)S(1)} %bitcast_add_fusion), channel_id=1, source_target_pairs={{0,4},{1,5},{2,6},{3,7},{4,0},{5,1},{6,2},{7,3},{8,12},{9,13},{10,... | collective-permute-start | bytes 1544 | tf_op jit(solution)/shard_map/ppermute | solution.py:339
